TPU v7x, 512 devices: a whole 4x8x8 slice. The times are simulated.
512 devices in a mesh: req: 64 (over z, x, core), tp: 8 (over y).
Axes of the slice: x: 4, y: 8, z: 8, core: 2. Of those that a mesh axis runs over, the one named last changes fastest.
Arguments:
- queries: bfloat16 [1024, 2560], P('req', 'tp'), may hold values from -64 to 64
- fresh_kv: bfloat16 [1024, 1280], P('req', 'tp'), may hold values from -9 to 9
- kv_cache: bfloat16 [8, 160, 655360], P('tp', None, 'req'), may hold values from -6 to 6
- out_weight: bfloat16 [2560, 2560], P('tp'), may hold values from -1.1953125 to 1.1953125
- offsets: int32 [1024], replicated, may hold values from 0 to 655358, as said below
- lengths: int32 [1024], replicated, may hold values from 2 to 8192, as said below
Outputs:
- mixed_out: bfloat16 [1024, 2560], P('req', 'tp')
Inputs may be any that keep to these rules, and one draw needn't show every extreme that they name: Request r belongs to index floor(r / 16) of req and its cache to index floor(offsets[r] / 10240), where it lies whole: offsets[r] + lengths[r] <= (floor(offsets[r] / 10240) + 1) * 10240; caches never intersect. The first 8 requests of each index have their caches on that index; every index holds the caches of exactly 8 requests of other indices, and those of one index's other requests lie on distinct indices. `lengths`: on every index of req one held cache has exactly 8192 tokens.
All inputs are finite; a program needn't handle non-finite values.
Results may differ from a plain program's by a relative error of at most 0.019.
Values may be sent and summed in bfloat16 or wider, within the bound.
No kernel may reach another device: no remote copies, remote signals or barrier semaphores. Data moves between devices by JAX's collectives and lax.ppermute only.
A program may use at most 64 MiB of HBM per device.

v0:
```python
import jax
import jax.numpy as jnp
from jax import lax
from jax.sharding import PartitionSpec as P

HD = 80
W = 4096


def attend(queries, fresh_kv, cache_block, starts, lengths):
    row_count = queries.shape[0]
    kv_heads = cache_block.shape[0]
    tokens = cache_block.shape[2]
    score_scale = HD ** (-0.5)
    grouped = queries.reshape(row_count, kv_heads, -1, HD)
    fresh_split = fresh_kv.reshape(row_count, kv_heads, 2, HD)
    scores = (
        jnp.einsum(
            "nhgd,hdt->hngt", grouped, cache_block[:, :HD, :], preferred_element_type=jnp.float32
        )
        * score_scale
    )
    positions = jnp.arange(tokens, dtype=jnp.int32)[None, :]
    window_end = (starts + lengths)[:, None]
    inside = (
        (positions >= starts[:, None])
        & (positions < window_end)
        & (positions >= window_end - (W - 1))
    )
    scores = jnp.where(inside[None, :, None, :], scores, -jnp.inf)
    own_score = (
        jnp.einsum(
            "nhgd,nhd->hng", grouped, fresh_split[:, :, 0, :], preferred_element_type=jnp.float32
        )
        * score_scale
    )
    highest = jnp.maximum(jnp.max(scores, axis=3), own_score)
    weights = jnp.exp(scores - highest[..., None])
    own_weight = jnp.exp(own_score - highest)
    totals = jnp.sum(weights, axis=3) + own_weight
    summed = jnp.einsum(
        "hngt,hdt->nhgd",
        weights.astype(jnp.bfloat16),
        cache_block[:, HD:, :],
        preferred_element_type=jnp.float32,
    )
    summed = summed + jnp.einsum(
        "hng,nhd->nhgd",
        own_weight.astype(jnp.bfloat16),
        fresh_split[:, :, 1, :],
        preferred_element_type=jnp.float32,
    )
    normed = summed / jnp.transpose(totals, (1, 0, 2))[..., None]
    return normed.astype(jnp.bfloat16).reshape(row_count, -1)


def shards(queries, fresh_kv, kv_cache, out_weight, offsets, lengths):
    devices = lax.axis_size("req")
    device_index = lax.axis_index("req")
    row_count = queries.shape[0]
    half_rows = row_count // 2
    shard_tokens = kv_cache.shape[2]
    shard_start = device_index * shard_tokens
    owner_table = (offsets // shard_tokens).reshape(devices, row_count)
    far_owners = owner_table[:, half_rows:]
    my_owners = lax.dynamic_slice_in_dim(far_owners, device_index, 1, 0)[0]
    home_first = device_index * row_count
    local_out = attend(
        queries[:half_rows],
        fresh_kv[:half_rows],
        kv_cache,
        lax.dynamic_slice_in_dim(offsets, home_first, half_rows) - shard_start,
        lax.dynamic_slice_in_dim(lengths, home_first, half_rows),
    )
    sent_queries, sent_fresh = (
        lax.all_gather(queries[half_rows:], "req", axis=0, tiled=True),
        lax.all_gather(fresh_kv[half_rows:], "req", axis=0, tiled=True),
    )
    flat_owners = far_owners.reshape(-1)
    picked = jnp.nonzero(flat_owners == device_index, size=half_rows)[0].astype(jnp.int32)
    request_ids = picked // half_rows * row_count + half_rows + picked % half_rows
    held_out = attend(
        jnp.take(sent_queries, picked, axis=0),
        jnp.take(sent_fresh, picked, axis=0),
        kv_cache,
        jnp.take(offsets, request_ids) - shard_start,
        jnp.take(lengths, request_ids),
    )
    returned = lax.all_gather(held_out, "req", axis=0, tiled=True)
    ordinal = device_index * half_rows + jnp.arange(half_rows, dtype=jnp.int32)
    earlier = jnp.arange(devices * half_rows, dtype=jnp.int32)[None, :] < ordinal[:, None]
    match_owner = flat_owners[None, :] == my_owners[:, None]
    rank_list = jnp.sum((earlier & match_owner).astype(jnp.int32), axis=1)
    remote_out = jnp.take(returned, my_owners * half_rows + rank_list, axis=0)
    attended = jnp.concatenate([local_out, remote_out], axis=0)
    partial_value = jnp.dot(attended, out_weight, preferred_element_type=jnp.float32)
    return lax.psum_scatter(
        partial_value.astype(jnp.bfloat16), "tp", scatter_dimension=1, tiled=True
    )


def solution(mesh):
    in_specs = (P("req", "tp"), P("req", "tp"), P("tp", None, "req"), P("tp", None), P(), P())
    out_specs = P("req", "tp")
    return jax.shard_map(shards, mesh=mesh, in_specs=in_specs, out_specs=out_specs, check_vma=False)
```

profile of v0, /device:TPU:1, one launch (start us, length us, event | category | flops | bytes accessed | tf_op | source)
XLA Modules:
  0.0 215.2 jit_solution(9321281883849411793)
XLA Ops:
  6.5 0.8 add_select_fusion
  7.4 0.7 fusion.70
  8.2 0.1 reshape.401
  8.3 0.3 reduce-window.12
  8.6 0.1 slice.49
  8.7 0.1 slice_reduce_fusion
  8.9 4.1 %scatter_custom_fusion = s32[8]{0:T(128)S(1)} fusion(s32[512]{0:T(512)S(1)} %bitcast.126, s32[512]{0:T(512)S(1)} %broadcast.332, s32[]{:T(128)} %constant.114.clone.1), kind=kCustom, calls=%fused_computation.118 | custom fusion | flops 512 | bytes 36 | tf_op jit(solution)/shard_map/scatter-add | solution.py:80
  13.0 0.2 select_n.123
  13.1 0.7 fusion.64
  13.8 0.7 compare_and_fusion.1
  14.5 0.7 fusion.72
  15.2 0.1 reshape.388
  15.3 0.7 fusion.71
  16.0 0.1 reshape.386
  16.1 0.1 fusion.55
  16.2 0.1 copy.31
  16.3 0.1 eq.29
  16.4 0.2 convert_reduce_fusion
  16.7 1.3 gather_fusion.1
  18.0 0.6 gather_fusion.2
  18.6 51.6 %all_gather.10 = bf16[512,160]{1,0:T(8,128)(2,1)S(1)} all-gather(bf16[8,160]{1,0:T(8,128)(2,1)S(1)} %get-tuple-element.23), channel_id=1, replica_groups=mesh['req'=64,'tp'=8] {'req'}, dimensions={0}, use_global_device_ids=true | all-gather | bytes 166400 | tf_op jit(solution)/shard_map/all_gather | solution.py:77
  70.3 0.6 gather_fusion
  70.9 0.1 gather.13
  70.9 0.1 copy_select_fusion
  71.0 46.6 %all_gather.9 = bf16[512,320]{1,0:T(8,128)(2,1)S(1)} all-gather(bf16[8,320]{1,0:T(8,128)(2,1)S(1)} %get-tuple-element.21), channel_id=1, replica_groups=mesh['req'=64,'tp'=8] {'req'}, dimensions={0}, use_global_device_ids=true | all-gather | bytes 332800 | tf_op jit(solution)/shard_map/all_gather | solution.py:76
  117.6 0.6 gather_fusion.3
  118.2 0.1 broadcast_select_fusion.1
  118.2 0.1 reshape.396
  118.3 0.1 fusion.56
  118.4 0.1 copy.33
  118.5 0.8 broadcast_add_fusion.1
  119.3 0.2 fusion.47
  119.5 2.0 fusion.73
  121.5 0.4 fusion.14
  121.9 0.6 fusion.37
  122.6 0.1 reshape.399
  122.7 46.7 %all_gather.11 = bf16[512,320]{1,0:T(8,128)(2,1)S(1)} all-gather(bf16[8,320]{1,0:T(8,128)(2,1)S(1)} %reshape.399), channel_id=1, replica_groups=mesh['req'=64,'tp'=8] {'req'}, dimensions={0}, use_global_device_ids=true | all-gather | bytes 332800 | tf_op jit(solution)/shard_map/all_gather | solution.py:89
  169.4 0.2 fusion.45
  169.5 2.0 fusion.74
  171.6 0.4 fusion.12
  172.0 0.6 fusion.34
  172.6 0.1 reshape.392
  172.7 0.6 gather_fusion.4
  173.3 0.1 broadcast_select_fusion
  173.4 0.3 convolution_convert_fusion
  173.7 1.1 copy.34
  174.8 31.9 %reduce-scatter.4.cloned.1.call-done = bf16[320,16]{1,0:T(8,128)(2,1)} async-done(((bf16[2560,16]{1,0:T(8,128)(2,1)}), bf16[320,16]{1,0:T(8,128)(2,1)}) %reduce-scatter.4.cloned.1.call-update) | async-done | bytes 10256
  206.8 1.6 copy.35
  (31 shorter events, 0.4 us)
Async XLA Ops:
  6.5 166.8 %copy-start = (bf16[320,2560]{1,0:T(8,128)(2,1)S(1)}, bf16[320,2560]{1,0:T(8,128)(2,1)}, u32[]{:S(2)}) copy-start(bf16[320,2560]{1,0:T(8,128)(2,1)} %param.13) | copy-start | bytes 4915204
  6.5 11.5 %copy-start.1 = (s32[1024]{0:T(1024)S(1)}, s32[1024]{0:T(1024)}, u32[]{:S(2)}) copy-start(s32[1024]{0:T(1024)} %param.15) | copy-start | bytes 12292
  6.5 200.3 %reduce-scatter.4.cloned.1.call-start = ((), (), s32[]{:S(2)}) async-start(), calls=%async_computation.1 | async-start | bytes 737280
  119.5 2.5 %copy-start.2 = (bf16[1,160,10240]{2,1,0:T(8,128)(2,1)S(1)}, bf16[1,160,10240]{2,1,0:T(8,128)(2,1)}, u32[]{:S(2)}) copy-start(bf16[1,160,10240]{2,1,0:T(8,128)(2,1)} %param.12) | copy-start | bytes 9830404
  169.5 2.5 %copy-start.3 = (bf16[1,160,10240]{2,1,0:T(8,128)(2,1)S(1)}, bf16[1,160,10240]{2,1,0:T(8,128)(2,1)}, u32[]{:S(2)}) copy-start(bf16[1,160,10240]{2,1,0:T(8,128)(2,1)} %param.12) | copy-start | bytes 9830404
Sparse Core Ops, SparseCore 0:
  175.0 31.7 reduce-scatter.3
where the time goes:
time: 219 us; the launch traced here: 215 us
  blocking collectives  145 us (66%)
  waiting for transfers between devices  32 us (15%)
  between operations  13.5 us (6%)
  other arithmetic  9.94 us (5%)
  local copies, waits for them, and re-layouts  8.91 us (4%)
  matrix products  5.93 us (3%)
    all_gather x1, blocking collectives, shards(): lax.all_gather(fresh_kv[half_rows:], 'req', axis=0, tiled=True)  51.6 us
    all_gather x1, blocking collectives, shards(): returned = lax.all_gather(held_out, 'req', axis=0, tiled=True)  46.7 us
    all_gather x1, blocking collectives, shards(): lax.all_gather(queries[half_rows:], 'req', axis=0, tiled=True)  46.6 us
    unnamed x2, waiting for transfers between devices  32 us
  transfers between devices with their start and end apart: 1, of which 1 were waited for; matrix products, arithmetic and copies ran while one was open for 0% of the time, Pallas kernels for 0%

commit v1 on v0

v1 whole, which is shorter than its diff:
```python
import jax
import jax.numpy as jnp
from jax import lax
from jax.sharding import PartitionSpec as P

HD = 80
W = 4096
MESSAGE = 512


def attend(queries, fresh_kv, cache_block, starts, lengths):
    row_count = queries.shape[0]
    kv_heads = cache_block.shape[0]
    tokens = cache_block.shape[2]
    score_scale = HD ** (-0.5)
    grouped = queries.reshape(row_count, kv_heads, -1, HD)
    fresh_split = fresh_kv.reshape(row_count, kv_heads, 2, HD)
    scores = (
        jnp.einsum(
            "nhgd,hdt->hngt", grouped, cache_block[:, :HD, :], preferred_element_type=jnp.float32
        )
        * score_scale
    )
    positions = jnp.arange(tokens, dtype=jnp.int32)[None, :]
    window_end = (starts + lengths)[:, None]
    inside = (
        (positions >= starts[:, None])
        & (positions < window_end)
        & (positions >= window_end - (W - 1))
    )
    scores = jnp.where(inside[None, :, None, :], scores, -jnp.inf)
    own_score = (
        jnp.einsum(
            "nhgd,nhd->hng", grouped, fresh_split[:, :, 0, :], preferred_element_type=jnp.float32
        )
        * score_scale
    )
    highest = jnp.maximum(jnp.max(scores, axis=3), own_score)
    weights = jnp.exp(scores - highest[..., None])
    own_weight = jnp.exp(own_score - highest)
    totals = jnp.sum(weights, axis=3) + own_weight
    summed = jnp.einsum(
        "hngt,hdt->nhgd",
        weights.astype(jnp.bfloat16),
        cache_block[:, HD:, :],
        preferred_element_type=jnp.float32,
    )
    summed = summed + jnp.einsum(
        "hng,nhd->nhgd",
        own_weight.astype(jnp.bfloat16),
        fresh_split[:, :, 1, :],
        preferred_element_type=jnp.float32,
    )
    normed = summed / jnp.transpose(totals, (1, 0, 2))[..., None]
    return normed.astype(jnp.bfloat16).reshape(row_count, -1)


def shards(queries, fresh_kv, kv_cache, out_weight, offsets, lengths):
    devices = lax.axis_size("req")
    columns = lax.axis_size("tp")
    device_index = lax.axis_index("req")
    row_count, width = queries.shape
    half_rows = row_count // 2
    shard_tokens = kv_cache.shape[2]
    home_first = device_index * row_count
    my_offsets = lax.dynamic_slice_in_dim(offsets, home_first, row_count)
    my_lengths = lax.dynamic_slice_in_dim(lengths, home_first, row_count)
    my_owners = my_offsets // shard_tokens
    my_starts = my_offsets - my_owners * shard_tokens
    slot = jnp.arange(devices, dtype=jnp.int32)
    placed = (slot[:, None] == my_owners[None, half_rows:]).astype(jnp.bfloat16)
    digits = jnp.stack(
        [
            jnp.ones_like(my_starts),
            my_starts >> 7,
            my_starts & 127,
            my_lengths >> 7,
            my_lengths & 127,
        ],
        axis=1,
    )
    digits = jnp.pad(digits, ((0, 0), (0, MESSAGE - 3 * width // 2 - 5)))
    message = jnp.concatenate([queries, fresh_kv, digits.astype(jnp.bfloat16)], axis=1)
    sent = jnp.dot(placed, message[half_rows:], preferred_element_type=jnp.float32)
    got = lax.all_to_all(sent.astype(jnp.bfloat16), "req", 0, 0, tiled=True)
    valid = got[:, 3 * width // 2] > 0.5
    rank = jnp.sum((slot[None, :] < slot[:, None]) & valid[None, :], axis=1)
    chosen = (
        (rank[:, None] == jnp.arange(half_rows)[None, :]) & valid[:, None]
    ).astype(jnp.bfloat16)
    held = lax.dot_general(
        chosen, got, (((0,), (0,)), ((), ())), preferred_element_type=jnp.float32
    )
    held_digits = held[:, 3 * width // 2 :].astype(jnp.int32)
    held_starts = held_digits[:, 1] * 128 + held_digits[:, 2]
    held_lengths = held_digits[:, 3] * 128 + held_digits[:, 4]
    held = held.astype(jnp.bfloat16)
    attended = attend(
        jnp.concatenate([queries[:half_rows], held[:, :width]], axis=0),
        jnp.concatenate([fresh_kv[:half_rows], held[:, width : 3 * width // 2]], axis=0),
        kv_cache,
        jnp.concatenate([my_starts[:half_rows], held_starts]),
        jnp.concatenate([my_lengths[:half_rows], held_lengths]),
    )
    partial_value = jnp.dot(attended, out_weight, preferred_element_type=jnp.float32)
    shares = partial_value.astype(jnp.bfloat16).reshape(row_count, columns, width)
    shares = lax.all_to_all(jnp.transpose(shares, (1, 0, 2)), "tp", 0, 0, tiled=True)
    mixed = jnp.sum(shares.astype(jnp.float32), axis=0).astype(jnp.bfloat16)
    spread = jnp.dot(chosen, mixed[half_rows:], preferred_element_type=jnp.float32)
    returned = lax.all_to_all(spread.astype(jnp.bfloat16), "req", 0, 0, tiled=True)
    far = lax.dot_general(
        placed, returned, (((0,), (0,)), ((), ())), preferred_element_type=jnp.float32
    )
    return jnp.concatenate([mixed[:half_rows], far.astype(jnp.bfloat16)], axis=0)


def solution(mesh):
    in_specs = (P("req", "tp"), P("req", "tp"), P("tp", None, "req"), P("tp", None), P(), P())
    out_specs = P("req", "tp")
    return jax.shard_map(shards, mesh=mesh, in_specs=in_specs, out_specs=out_specs, check_vma=False)
```

time: 219 us -> 68 us (0.31); the launches traced: 215 us -> 67.6 us
  blocking collectives: 145 us -> 14.1 us
  starting transfers between devices: 0.01 us -> 20.9 us
  between operations: 13.5 us -> 0.22 us
  waiting for transfers between devices: 32 us -> 18.8 us
  other arithmetic: 9.94 us -> 4.36 us
  local copies, waits for them, and re-layouts: 8.91 us -> 4.24 us
    all_gather x3 -> x0, blocking collectives: 145 us -> none  [the longest x1 51.6 us: shards(): lax.all_gather(fresh_kv[half_rows:], 'req', axis=0, tiled=True)]
    unnamed x2 -> x0, waiting for transfers between devices: 32 us -> none
    all_to_all x0 -> x2, starting transfers between devices: none -> 20.9 us  [the longest x1 14.8 us: shards(): got = lax.all_to_all(sent.astype(jnp.bfloat16), 'req', 0, 0, tiled=True)]
    all_to_all x0 -> x2, waiting for transfers between devices: none -> 18.8 us  [the longest x1 10.1 us: shards(): lax.all_to_all(spread.astype(jnp.bfloat16), 'req', 0, 0, tiled=True)]
    all_to_all x0 -> x1, blocking collectives: none -> 14.1 us  [shards(): lax.all_to_all(jnp.transpose(shares, (1, 0, 2)), 'tp', 0, 0, tiled=True)]
    scatter-add x1 -> x0, other arithmetic: 4.09 us -> none  [shards(): jnp.nonzero(flat_owners == device_index, size=half_rows)[0]]
    gather x6 -> x0, local copies, waits for them, and re-layouts: 3.76 us -> none  [the longest x1 1.33 us: shards(): jnp.take(offsets, request_ids) - shard_start]
  transfers between devices with their start and end apart: 1 -> 2, of which waited for: 1 -> 2; matrix products, arithmetic and copies ran while one was open for 0% -> 2% of each run, Pallas kernels for 0% -> 0%
where the time goes in v1:
time: 68 us; the launch traced here: 67.6 us
  starting transfers between devices  20.9 us (31%)
  waiting for transfers between devices  18.8 us (28%)
  blocking collectives  14.1 us (21%)
  matrix products  4.95 us (7%)
  other arithmetic  4.36 us (6%)
  local copies, waits for them, and re-layouts  4.24 us (6%)
    all_to_all x1, starting transfers between devices, shards(): got = lax.all_to_all(sent.astype(jnp.bfloat16), 'req', 0, 0, tiled=True)  14.8 us
    all_to_all x1, blocking collectives, shards(): lax.all_to_all(jnp.transpose(shares, (1, 0, 2)), 'tp', 0, 0, tiled=True)  14.1 us
    all_to_all x1, waiting for transfers between devices, shards(): lax.all_to_all(spread.astype(jnp.bfloat16), 'req', 0, 0, tiled=True)  10.1 us
    all_to_all x1, waiting for transfers between devices, shards(): got = lax.all_to_all(sent.astype(jnp.bfloat16), 'req', 0, 0, tiled=True)  8.7 us
    all_to_all x1, starting transfers between devices, shards(): lax.all_to_all(spread.astype(jnp.bfloat16), 'req', 0, 0, tiled=True)  6.04 us
    dot_general x1, matrix products, attend(): jnp.einsum('nhgd,hdt->hngt', grouped, cache_block[:, :HD, :], preferred_e...  2.22 us
    unnamed x11, local copies, waits for them, and re-layouts  1.65 us
  transfers between devices with their start and end apart: 2, of which 2 were waited for; matrix products, arithmetic and copies ran while one was open for 2% of the time, Pallas kernels for 0%

profile of v1, /device:TPU:1, one launch (start us, length us, event | category | flops | bytes accessed | tf_op | source)
XLA Modules:
  0.0 67.6 jit_solution(13107287592061188868)
XLA Ops:
  0.0 0.0 copy-start
  0.0 0.9 %convert_bitcast_fusion = (bf16[16,1]{0,1:T(2,128)(2,1)S(1)}, s32[16]{0:T(128)S(1)}, bf16[16,1]{0,1:T(2,128)(2,1)S(1)}, s32[16]{0:T(128)S(1)}, s32[16]{0:T(128)S(1)}) fusion(s32[1024]{0:T(1024)} %param.11, s32[]{:T(128)S(6)} %select_n.14, s32[1024]{0:T(1024)} %param.10), kind=kLoop, calls=%fused_computation.71 | loop fusion | flops 224 | bytes 388 | tf_op jit(solution)/shard_map/stack | solution.py:72
  1.0 0.1 copy.39
  1.1 0.1 slice.61
  1.2 0.9 %fusion.10 = bf16[64,1,512]{2,0,1:T(8,128)(2,1)S(1)} fusion(s32[8]{0:T(128)S(1)} %slice.61, bf16[16,5]{1,0:T(8,128)(2,1)S(1)} %copy.39, bf16[16,160]{1,0:T(8,128)(2,1)} %param.7, bf16[16,320]{1,0:T(8,128)(2,1)} %param.6), kind=kOutput, calls=%fused_computation.14 | convolution fusion | flops 590336 | bytes 81088 | tf_op jit(solution)/shard_map/dot_general | solution.py:84
  2.1 0.5 broadcast.120
  2.6 0.7 reduce.11
  3.3 0.6 reshape.202
  3.9 14.8 %all-to-all-start = ((bf16[64,2,256]{2,1,0:T(2,128)(2,1)}), bf16[64,2,256]{2,1,0:T(2,128)(2,1)S(1)}, u32[]{:S(2)}, u32[]{:S(2)}) async-start(bf16[64,2,256]{2,1,0:T(2,128)(2,1)} %reshape.202), calls=%async_computation | async-start | bytes 131072 | tf_op jit(solution)/shard_map/all_to_all | solution.py:85
  18.7 0.7 %slice.70 = bf16[8,320]{1,0:T(8,128)(2,1)S(1)} slice(bf16[16,320]{1,0:T(8,128)(2,1)} %param.6), slice={[0:8], [0:320]} | slice | bytes 10240 | tf_op jit(solution)/shard_map/slice | solution.py:99
  19.4 0.7 %slice.73 = bf16[8,160]{1,0:T(8,128)(2,1)S(1)} slice(bf16[16,160]{1,0:T(8,128)(2,1)} %param.7), slice={[0:8], [0:160]} | slice | bytes 5120 | tf_op jit(solution)/shard_map/slice | solution.py:100
  20.1 8.7 %all-to-all-done = bf16[64,2,256]{2,1,0:T(2,128)(2,1)S(1)} async-done(((bf16[64,2,256]{2,1,0:T(2,128)(2,1)}), bf16[64,2,256]{2,1,0:T(2,128)(2,1)S(1)}, u32[]{:S(2)}, u32[]{:S(2)}) %all-to-all-start) | async-done | bytes 65568 | tf_op jit(solution)/shard_map/all_to_all | solution.py:85
  28.8 0.1 reshape.203
  28.9 0.2 compare_reduce_fusion
  29.1 0.1 convert_reduce_fusion
  29.2 0.3 fusion.63
  29.5 0.1 slice.83
  29.5 0.1 slice_convert_fusion.1
  29.6 0.2 add_reduce_fusion
  29.8 0.1 reshape.186
  29.9 0.1 reshape.188
  30.0 0.1 fusion.54
  30.2 0.1 copy.35
  30.2 0.1 broadcast_add_fusion
  30.3 0.3 fusion.33
  30.6 0.0 copy-start.1
  30.6 2.2 %fusion.64 = (f32[16,4]{0,1:T(4,128)S(1)}, f32[16,4,10240]{2,0,1:T(8,128)S(1)}) fusion(bf16[1,160,10240]{2,1,0:T(8,128)(2,1)} %param.8, bf16[16,4,80]{2,1,0:T(4,128)(2,1)S(1)} %reshape.186, pred[16,10240]{1,0:T(8,128)(4,1)S(1)} %fusion.33), kind=kOutput, calls=%fused_computation.82 | convolution fusion | flops 106823616 | bytes 4434176 | tf_op jit(solution)/shard_map/nhgd,hdt->hngt/dot_general | solution.py:19
  32.8 0.5 fusion.1
  33.4 0.0 copy-done.1
  33.4 0.7 %fusion.27 = bf16[16,1,4,80]{3,0,2,1:T(8,128)(2,1)S(1)} fusion(bf16[1,160,10240]{2,1,0:T(8,128)(2,1)S(1)} %copy-done.1, f32[16,4,10240]{2,0,1:T(8,128)S(1)} %get-tuple-element.22, f32[16,4]{0,1:T(4,128)S(1)} %fusion.58, f32[16,4]{0,1:T(4,128)S(1)} %get-tuple-element.18, f32[16,80]{1,0:T(8,128)S(1)} %bitcast.84, f32[16,4]{0,1:T(4,128)S(1)} %get-tuple-element.17), kind=kOutput, calls=%fused_computation.19 | convolution fusion | flops 106188800 | bytes 4284416 | tf_op jit(solution)/shard_map/hngt,hdt->nhgd/dot_general | solution.py:42
  34.1 0.1 reshape.192
  34.2 0.0 copy-done
  34.2 0.3 convolution_convert_fusion
  34.6 0.1 reshape.193
  34.8 14.1 %all_to_all.29 = bf16[8,16,320]{2,1,0:T(8,128)(2,1)S(1)} all-to-all(bf16[8,16,320]{2,1,0:T(8,128)(2,1)S(1)} %bitcast.81), channel_id=1, replica_groups=mesh['req'=64,'tp'=8] {'tp'}, dimensions={0} | all-to-all | bytes 163840 | tf_op jit(solution)/shard_map/all_to_all | solution.py:107
  48.9 0.2 fusion.11
  49.1 0.7 reduce.12
  49.7 0.7 %reshape.204 = bf16[64,2,160]{2,1,0:T(2,128)(2,1)} reshape(bf16[64,320]{1,0:T(8,128)(2,1)S(1)} %reduce.12) | data formatting | bytes 81920
  50.5 6.0 %all-to-all-start.2 = ((bf16[64,2,160]{2,1,0:T(2,128)(2,1)}), bf16[64,2,160]{2,1,0:T(2,128)(2,1)S(1)}, u32[]{:S(2)}, u32[]{:S(2)}) async-start(bf16[64,2,160]{2,1,0:T(2,128)(2,1)} %reshape.204), calls=%async_computation.2 | async-start | bytes 131072 | tf_op jit(solution)/shard_map/all_to_all | solution.py:110
  56.5 10.1 %all-to-all-done.2 = bf16[64,2,160]{2,1,0:T(2,128)(2,1)S(1)} async-done(((bf16[64,2,160]{2,1,0:T(2,128)(2,1)}), bf16[64,2,160]{2,1,0:T(2,128)(2,1)S(1)}, u32[]{:S(2)}, u32[]{:S(2)}) %all-to-all-start.2) | async-done | bytes 40992 | tf_op jit(solution)/shard_map/all_to_all | solution.py:110
  66.6 0.1 reshape.205
  66.8 0.2 convolution_convert_fusion.3
  66.9 0.6 pad_maximum_fusion.1
  (16 shorter events, 0.2 us)
Async XLA Ops:
  0.0 34.2 %copy-start = (bf16[320,2560]{1,0:T(8,128)(2,1)S(1)}, bf16[320,2560]{1,0:T(8,128)(2,1)}, u32[]{:S(2)}) copy-start(bf16[320,2560]{1,0:T(8,128)(2,1)} %param.9) | copy-start | bytes 4915204
  3.9 24.9 %all-to-all-start = ((bf16[64,2,256]{2,1,0:T(2,128)(2,1)}), bf16[64,2,256]{2,1,0:T(2,128)(2,1)S(1)}, u32[]{:S(2)}, u32[]{:S(2)}) async-start(bf16[64,2,256]{2,1,0:T(2,128)(2,1)} %reshape.202), calls=%async_computation | async-start | bytes 131072 | tf_op jit(solution)/shard_map/all_to_all | solution.py:85
  30.6 2.8 %copy-start.1 = (bf16[1,160,10240]{2,1,0:T(8,128)(2,1)S(1)}, bf16[1,160,10240]{2,1,0:T(8,128)(2,1)}, u32[]{:S(2)}) copy-start(bf16[1,160,10240]{2,1,0:T(8,128)(2,1)} %param.8) | copy-start | bytes 9830404
  50.5 16.2 %all-to-all-start.2 = ((bf16[64,2,160]{2,1,0:T(2,128)(2,1)}), bf16[64,2,160]{2,1,0:T(2,128)(2,1)S(1)}, u32[]{:S(2)}, u32[]{:S(2)}) async-start(bf16[64,2,160]{2,1,0:T(2,128)(2,1)} %reshape.204), calls=%async_computation.2 | async-start | bytes 131072 | tf_op jit(solution)/shard_map/all_to_all | solution.py:110

commit v2 on v0

v2 whole, which is shorter than its diff:
```python
import functools

import jax
import jax.numpy as jnp
from jax import lax
from jax.experimental import pallas as pl
from jax.experimental.pallas import tpu as pltpu
from jax.sharding import PartitionSpec as P

HD = 80
G = 4
W = 4096
LMAX = 8192
LANES = 128
BF = jnp.bfloat16
F32 = jnp.float32
I32 = jnp.int32
VMEM = pl.BlockSpec(memory_space=pltpu.VMEM)


def iota(shape, axis):
    return lax.broadcasted_iota(I32, shape, axis)


def dot(a, b):
    return jnp.dot(a, b, preferred_element_type=F32)


def dot_t(a, b):
    return lax.dot_general(a, b, (((1,), (1,)), ((), ())), preferred_element_type=F32)


def own_row(table_ref, index, shift):
    per_row = LANES // 16
    row = table_ref[pl.ds(index // per_row, 1), :]
    back = (index % per_row) * 16 + shift
    return pltpu.roll(row, (LANES - back) % LANES, 1)


def column(row, count):
    wide = jnp.broadcast_to(row, (count, LANES))
    same = iota((count, LANES), 0) == iota((count, LANES), 1)
    return jnp.sum(jnp.where(same, wide, 0), axis=1, keepdims=True)


def slot_matrix(offsets_ref, index, tokens, slots):
    owners = own_row(offsets_ref, index, 8) // tokens
    lane = iota((1, LANES), 1)
    spread = jnp.where(lane < 8, owners, 0)
    spread = spread + jnp.where((lane >= 8) & (lane < 16), pltpu.roll(owners, 8, 1), 0)
    spread = spread + jnp.where((lane >= 16) & (lane < 24), pltpu.roll(owners, 16, 1), 0)
    spread = spread + jnp.where((lane >= 24) & (lane < 32), pltpu.roll(owners, 24, 1), 0)
    row = iota((slots * 4, LANES), 0)
    col = iota((slots * 4, LANES), 1)
    hit = ((row >> 2) == jnp.broadcast_to(spread, (slots * 4, LANES))) & ((row & 3) == (col >> 3))
    return jnp.where(hit, 1.0, 0.0).astype(BF)


def send_kernel(tokens, offsets_ref, lengths_ref, queries_ref, fresh_ref, out_ref):
    index = lax.axis_index("req")
    slots = out_ref.shape[0] // 4
    placed = slot_matrix(offsets_ref, index, tokens, slots)
    starts = column(own_row(offsets_ref, index, 8) % tokens, 8)
    lengths = column(own_row(lengths_ref, index, 8), 8)
    queries = queries_ref[...].astype(F32)[8:]
    fresh = fresh_ref[...].astype(F32)[8:]
    lane = iota((8, LANES), 1)
    meta = jnp.where(lane == 96, 1, 0)
    meta = jnp.where(lane == 97, starts >> 7, meta)
    meta = jnp.where(lane == 98, starts & 127, meta)
    meta = jnp.where(lane == 99, lengths >> 7, meta)
    meta = jnp.where(lane == 100, lengths & 127, meta)
    third = jnp.concatenate(
        [queries[:, 256:], fresh[:, 128:], jnp.zeros((8, 32), F32)], axis=1
    ) + meta.astype(F32)
    stack = jnp.concatenate(
        [queries[:, :128], queries[:, 128:256], third, fresh[:, :128], jnp.zeros((96, LANES), F32)],
        axis=0,
    )
    out_ref[...] = dot(placed, stack.astype(BF)).astype(BF)


def attend_kernel(
    tokens, offsets_ref, lengths_ref, queries_ref, fresh_ref, got_ref, cache_ref, weight_ref, out_ref, chosen_ref
):
    index = lax.axis_index("req")
    rows = got_ref.shape[0]
    scale = HD ** (-0.5)
    got = got_ref[...]
    flag = jnp.where(
        (iota((rows, LANES), 1) == 96) & ((iota((rows, LANES), 0) & 3) == 2), got.astype(F32), 0.0
    )
    flag = jnp.sum(flag, axis=1, keepdims=True)
    flags = jnp.broadcast_to(flag, (rows, LANES)).astype(BF)
    slot_a = iota((rows, rows), 0) >> 2
    slot_b = iota((rows, rows), 1) >> 2
    valid = dot(jnp.where(slot_a == slot_b, 1.0, 0.0).astype(BF), flags)
    rank = dot(jnp.where(slot_b < slot_a, 1.0, 0.0).astype(BF), flags)
    row = iota((rows, LANES), 0)
    col = iota((rows, LANES), 1)
    hit = (valid > 0.5) & (rank.astype(I32) == (col & 7)) & ((row & 3) == (col >> 3))
    chosen = jnp.where(hit, 1.0, 0.0)
    chosen_ref[...] = chosen.astype(BF)
    held = dot(jnp.transpose(chosen).astype(BF), got)
    meta = held[16:24]
    held_starts = (meta[:, 97:98] * 128.0 + meta[:, 98:99]).astype(I32)
    held_lengths = (meta[:, 99:100] * 128.0 + meta[:, 100:101]).astype(I32)
    held_queries = jnp.concatenate([held[0:8], held[8:16], held[16:24, :64]], axis=1)
    held_fresh = jnp.concatenate([held[24:32], held[16:24, 64:96]], axis=1)
    starts = column(own_row(offsets_ref, index, 0), 8) - index * tokens
    lengths = column(own_row(lengths_ref, index, 0), 8)
    starts = jnp.concatenate([starts, held_starts], axis=0)
    lengths = jnp.concatenate([lengths, held_lengths], axis=0)
    queries = jnp.concatenate([queries_ref[...].astype(F32)[:8], held_queries], axis=0)
    fresh = jnp.concatenate([fresh_ref[...].astype(F32)[:8], held_fresh], axis=0)
    fresh_key, fresh_value = fresh[:, :HD], fresh[:, HD : 2 * HD]
    heads = [queries[:, g * HD : (g + 1) * HD] for g in range(G)]
    own = [jnp.sum(h * fresh_key, axis=1, keepdims=True) * scale for h in heads]
    stacked = jnp.concatenate(heads, axis=0).astype(BF)
    own_all = jnp.concatenate(own, axis=0)
    is_long = lengths == LMAX
    long_start = jnp.sum(jnp.where(is_long, starts, 0))
    sub = iota((8, HD), 0)
    long_query = jnp.zeros((8, HD), F32)
    long_own = jnp.zeros((8, 1), F32)
    for g in range(G):
        picked = jnp.sum(jnp.where(is_long, heads[g], 0.0), axis=0, keepdims=True)
        long_query = jnp.where(sub == g, picked, long_query)
        picked_own = jnp.sum(jnp.where(is_long, own[g], 0.0), axis=0, keepdims=True)
        long_own = jnp.where(iota((8, 1), 0) == g, picked_own, long_own)
    long_value = jnp.sum(jnp.where(is_long, fresh_value, 0.0), axis=0, keepdims=True)
    span = W + LANES
    first = long_start + (LMAX - W + 1)
    base = jnp.minimum(first // LANES * LANES, tokens - span)
    window = pl.ds(pl.multiple_of(base, LANES), span)
    scores = dot(long_query.astype(BF), cache_ref[:HD, window]) * scale
    position = base + iota((8, span), 1)
    scores = jnp.where((position >= first) & (position < first + (W - 1)), scores, -jnp.inf)
    highest = jnp.maximum(jnp.max(scores, axis=1, keepdims=True), long_own)
    weights = jnp.exp(scores - highest)
    own_weight = jnp.exp(long_own - highest)
    totals = jnp.sum(weights, axis=1, keepdims=True) + own_weight
    summed = dot_t(weights.astype(BF), cache_ref[HD : 2 * HD, window])
    summed = summed + own_weight.astype(BF).astype(F32) * long_value
    long_out = summed / totals
    blocks = (tokens - LMAX) // LANES + 1
    before = (long_start + LANES - 1) // LANES
    after = (long_start + LMAX) // LANES
    last = tokens // LANES - 1
    keys, values, places = [], [], []
    for i in range(blocks):
        block = jnp.where(i < before, i, after + i - before)
        spare = block > last
        begin = pl.multiple_of(jnp.minimum(block, last) * LANES, LANES)
        keys.append(cache_ref[:HD, pl.ds(begin, LANES)])
        values.append(cache_ref[HD : 2 * HD, pl.ds(begin, LANES)])
        places.append(jnp.where(spare, -LANES, begin) + iota((1, LANES), 1))
    keys = jnp.concatenate(keys, axis=1)
    values = jnp.concatenate(values, axis=1)
    position = jnp.concatenate(places, axis=1)
    ends = starts + lengths
    firsts = jnp.maximum(starts, ends - (W - 1))
    ends = jnp.concatenate([ends] * G, axis=0)
    firsts = jnp.concatenate([firsts] * G, axis=0)
    scores = dot(stacked, keys) * scale
    scores = jnp.where((position >= firsts) & (position < ends), scores, -jnp.inf)
    highest = jnp.maximum(jnp.max(scores, axis=1, keepdims=True), own_all)
    weights = jnp.exp(scores - highest)
    own_weight = jnp.exp(own_all - highest)
    totals = jnp.sum(weights, axis=1, keepdims=True) + own_weight
    summed = dot_t(weights.astype(BF), values)
    summed = summed + own_weight.astype(BF).astype(F32) * jnp.concatenate([fresh_value] * G, axis=0)
    outs = summed / totals
    count = starts.shape[0]
    attended = [
        jnp.where(is_long, long_out[g : g + 1], outs[g * count : (g + 1) * count]) for g in range(G)
    ]
    attended = jnp.concatenate(attended, axis=1).astype(BF)
    width = G * HD
    for j in range(out_ref.shape[0]):
        left = j * width // LANES * LANES
        out_ref[j] = dot(attended, weight_ref[:, left : left + out_ref.shape[2]]).astype(BF)


def spread_kernel(shares_ref, chosen_ref, home_ref, out_ref):
    odd = (lax.axis_index("tp") % 2) == 1
    total = jnp.sum(shares_ref[...].astype(F32), axis=0)
    moved = jnp.concatenate([total[:, 64:], total[:, :64]], axis=1)
    mixed = jnp.where(odd, moved, total).astype(BF).astype(F32)
    home_ref[...] = mixed[:8, : home_ref.shape[1]].astype(BF)
    far = mixed[8:]
    stack = jnp.concatenate(
        [far[:, :128], far[:, 128:256], far[:, 256:], jnp.zeros((104, LANES), F32)], axis=0
    )
    out_ref[...] = dot(chosen_ref[...], stack.astype(BF)).astype(BF)


def pick_kernel(tokens, offsets_ref, home_ref, returned_ref, out_ref):
    index = lax.axis_index("req")
    placed = slot_matrix(offsets_ref, index, tokens, returned_ref.shape[0] // 4)
    far = dot(jnp.transpose(placed.astype(F32)).astype(BF), returned_ref[...])
    far = jnp.concatenate([far[0:8], far[8:16], far[16:24, :64]], axis=1)
    out_ref[...] = jnp.concatenate([home_ref[...].astype(F32), far], axis=0).astype(BF)


def call(kernel, out_shape, *args):
    return pl.pallas_call(
        kernel,
        out_shape=out_shape,
        in_specs=[VMEM] * len(args),
        out_specs=jax.tree.map(lambda _: VMEM, out_shape),
    )(*args)


def shards(queries, fresh_kv, kv_cache, out_weight, offsets, lengths):
    devices = lax.axis_size("req")
    columns = lax.axis_size("tp")
    row_count, width = queries.shape
    tokens = kv_cache.shape[2]
    cache = kv_cache.reshape(kv_cache.shape[1:])
    offsets = offsets.reshape(-1, LANES)
    lengths = lengths.reshape(-1, LANES)
    shape = jax.ShapeDtypeStruct
    slots = shape((devices * 4, LANES), BF)
    message = call(
        functools.partial(send_kernel, tokens), slots, offsets, lengths, queries, fresh_kv
    )
    got = lax.all_to_all(message.reshape(devices, 4, LANES), "req", 0, 0, tiled=True)
    shares, chosen = call(
        functools.partial(attend_kernel, tokens),
        (shape((columns, row_count, 384), BF), slots),
        offsets, lengths, queries, fresh_kv, got.reshape(devices * 4, LANES), cache, out_weight,
    )
    shares = lax.all_to_all(shares, "tp", 0, 0, tiled=True)
    home, spread = call(
        spread_kernel, (shape((row_count // 2, width), BF), slots), shares, chosen
    )
    returned = lax.all_to_all(spread.reshape(devices, 4, LANES), "req", 0, 0, tiled=True)
    return call(
        functools.partial(pick_kernel, tokens),
        shape((row_count, width), BF),
        offsets, home, returned.reshape(devices * 4, LANES),
    )


def solution(mesh):
    in_specs = (P("req", "tp"), P("req", "tp"), P("tp", None, "req"), P("tp", None), P(), P())
    out_specs = P("req", "tp")
    return jax.shard_map(shards, mesh=mesh, in_specs=in_specs, out_specs=out_specs, check_vma=False)
```

time: 219 us -> 67.4 us (0.31); the launches traced: 215 us -> 67 us
  blocking collectives: 145 us -> 56.3 us
  waiting for transfers between devices: 32 us -> 0 us
  between operations: 13.5 us -> 0.01 us
  Pallas kernels: 0 us -> 10.7 us
  other arithmetic: 9.94 us -> 0 us
  local copies, waits for them, and re-layouts: 8.91 us -> 0 us
  matrix products: 5.93 us -> 0 us
    all_gather x3 -> x0, blocking collectives: 145 us -> none  [the longest x1 51.6 us: shards(): lax.all_gather(fresh_kv[half_rows:], 'req', axis=0, tiled=True)]
    all_to_all x0 -> x3, blocking collectives: none -> 56.3 us  [the longest x1 25 us: shards(): lax.all_to_all(message.reshape(devices, 4, LANES), 'req', 0, 0, tiled=True)]
    unnamed x2 -> x0, waiting for transfers between devices: 32 us -> none
    pallas_call x0 -> x4, Pallas kernels: none -> 10.7 us  [call(): pl.pallas_call(kernel, out_shape=out_shape, in_specs=[VMEM] * len(args),...]
    dot_general x7 -> x0, matrix products: 5.93 us -> none  [the longest x2 4.07 us: attend(): jnp.einsum('nhgd,hdt->hngt', grouped, cache_block[:, :HD, :], preferred_e...]
    scatter-add x1 -> x0, other arithmetic: 4.09 us -> none  [shards(): jnp.nonzero(flat_owners == device_index, size=half_rows)[0]]
    gather x6 -> x0, local copies, waits for them, and re-layouts: 3.76 us -> none  [the longest x1 1.33 us: shards(): jnp.take(offsets, request_ids) - shard_start]
    unnamed x10 -> x0, local copies, waits for them, and re-layouts: 2.67 us -> none
  transfers between devices with their start and end apart: 1 -> 0, of which waited for: 1 -> 0; matrix products, arithmetic and copies ran while one was open for 0% -> 0% of each run, Pallas kernels for 0% -> 0%
where the time goes in v2:
time: 67.4 us; the launch traced here: 67 us
  blocking collectives  56.3 us (84%)
  Pallas kernels  10.7 us (16%)
    all_to_all x1, blocking collectives, shards(): lax.all_to_all(message.reshape(devices, 4, LANES), 'req', 0, 0, tiled=True)  25 us
    all_to_all x1, blocking collectives, shards(): lax.all_to_all(spread.reshape(devices, 4, LANES), 'req', 0, 0, tiled=True)  16.9 us
    all_to_all x1, blocking collectives, shards(): shares = lax.all_to_all(shares, 'tp', 0, 0, tiled=True)  14.4 us
    pallas_call x4, Pallas kernels, call(): pl.pallas_call(kernel, out_shape=out_shape, in_specs=[VMEM] * len(args),...  10.7 us

profile of v2, /device:TPU:1, one launch (start us, length us, event | category | flops | bytes accessed | tf_op | source)
XLA Modules:
  0.0 67.0 jit_solution(11708761582233650202)
XLA Ops:
  0.0 1.7 %shard_map.64 = bf16[256,128]{1,0:T(8,128)(2,1)} custom-call(s32[8,128]{1,0:T(8,128)} %bitcast.12, s32[8,128]{1,0:T(8,128)} %bitcast.15, bf16[16,320]{1,0:T(8,128)(2,1)} %queries_ref.3, bf16[16,160]{1,0:T(8,128)(2,1)} %fresh_ref.3), custom_call_target="tpu_custom_call" | custom-call | tf_op jit(solution)/shard_map/pallas_call | solution.py:207
  1.7 25.0 %all_to_all.15 = bf16[64,4,128]{2,1,0:T(4,128)(2,1)} all-to-all(bf16[64,4,128]{2,1,0:T(4,128)(2,1)} %bitcast.10), channel_id=1, replica_groups=mesh['req'=64,'tp'=8] {'req'}, dimensions={0} | all-to-all | bytes 131072 | tf_op jit(solution)/shard_map/all_to_all | solution.py:228
  26.7 5.5 %shard_map.65 = (bf16[8,16,384]{2,1,0:T(8,128)(2,1)}, bf16[256,128]{1,0:T(8,128)(2,1)}) custom-call(s32[8,128]{1,0:T(8,128)} %bitcast.13, s32[8,128]{1,0:T(8,128)} %bitcast.16, bf16[16,320]{1,0:T(8,128)(2,1)} %queries_ref.3, bf16[16,160]{1,0:T(8,128)(2,1)} %fresh_ref.3, bf16[256,128]{1,0:T(8,128)(2,1)} %bitcast.8, bf16[160,10240]{1,0:T(8,128)(2,1)} %bitcast.7, ...), custom_call_target="tpu_custom_call" | custom-call | tf_op jit(solution)/shard_map/pallas_call | solution.py:207
  32.2 14.4 %all_to_all.16.shares_ref = bf16[8,16,384]{2,1,0:T(8,128)(2,1)} all-to-all(bf16[8,16,384]{2,1,0:T(8,128)(2,1)} %get-tuple-element.9), channel_id=1, replica_groups=mesh['req'=64,'tp'=8] {'tp'}, dimensions={0} | all-to-all | bytes 196608 | tf_op jit(solution)/shard_map/all_to_all | solution.py:234
  46.6 1.7 %shard_map.66 = (bf16[8,320]{1,0:T(8,128)(2,1)}, bf16[256,128]{1,0:T(8,128)(2,1)}) custom-call(bf16[8,16,384]{2,1,0:T(8,128)(2,1)} %all_to_all.16.shares_ref, bf16[256,128]{1,0:T(8,128)(2,1)} %get-tuple-element.10.chosen_ref), custom_call_target="tpu_custom_call" | custom-call | tf_op jit(solution)/shard_map/pallas_call | solution.py:207
  48.3 16.9 %all_to_all.17 = bf16[64,4,128]{2,1,0:T(4,128)(2,1)} all-to-all(bf16[64,4,128]{2,1,0:T(4,128)(2,1)} %bitcast.11), channel_id=1, replica_groups=mesh['req'=64,'tp'=8] {'req'}, dimensions={0} | all-to-all | bytes 131072 | tf_op jit(solution)/shard_map/all_to_all | solution.py:238
  65.2 1.8 %shard_map.67 = bf16[16,320]{1,0:T(8,128)(2,1)} custom-call(s32[8,128]{1,0:T(8,128)} %bitcast.14, bf16[8,320]{1,0:T(8,128)(2,1)} %get-tuple-element.11.home_ref, bf16[256,128]{1,0:T(8,128)(2,1)} %bitcast.9), custom_call_target="tpu_custom_call" | custom-call | tf_op jit(solution)/shard_map/pallas_call | solution.py:207

commit v3 on v2

v3 whole, which is shorter than its diff:
```python
import functools

import jax
import jax.numpy as jnp
from jax import lax
from jax.experimental import pallas as pl
from jax.experimental.pallas import tpu as pltpu
from jax.sharding import PartitionSpec as P

HD = 80
G = 4
W = 4096
LMAX = 8192
LANES = 128
HALF = 8
BF = jnp.bfloat16
F32 = jnp.float32
I32 = jnp.int32
NEAR = pl.BlockSpec(memory_space=pltpu.VMEM)
ANYWHERE = pl.BlockSpec(memory_space=pltpu.HBM)


def iota(shape, axis):
    return lax.broadcasted_iota(I32, shape, axis)


def dot(a, b):
    return jnp.dot(a, b, preferred_element_type=F32)


def dot_t(a, b):
    return lax.dot_general(a, b, (((1,), (1,)), ((), ())), preferred_element_type=F32)


def own_row(table_ref, index, shift):
    per_row = LANES // 16
    row = table_ref[pl.ds(index // per_row, 1), :]
    back = (index % per_row) * 16 + shift
    return pltpu.roll(row, (LANES - back) % LANES, 1)


def column(row, count):
    wide = jnp.broadcast_to(row, (count, LANES))
    same = iota((count, LANES), 0) == iota((count, LANES), 1)
    return jnp.sum(jnp.where(same, wide, 0), axis=1, keepdims=True)


def pack(queries, fresh, starts, lengths):
    lane = iota((HALF, LANES), 1)
    meta = jnp.where(lane == 96, 1, 0)
    meta = jnp.where(lane == 97, starts >> 7, meta)
    meta = jnp.where(lane == 98, starts & 127, meta)
    meta = jnp.where(lane == 99, lengths >> 7, meta)
    meta = jnp.where(lane == 100, lengths & 127, meta)
    third = jnp.concatenate([queries[:, 256:], fresh[:, 128:], jnp.zeros((HALF, 32), F32)], axis=1)
    return jnp.concatenate(
        [queries[:, :128], queries[:, 128:256], third + meta.astype(F32), fresh[:, :128]], axis=0
    )


def unpack(stack):
    meta = stack[16:24]
    starts = (meta[:, 97:98] * 128.0 + meta[:, 98:99]).astype(I32)
    lengths = (meta[:, 99:100] * 128.0 + meta[:, 100:101]).astype(I32)
    queries = jnp.concatenate([stack[0:8], stack[8:16], stack[16:24, :64]], axis=1)
    fresh = jnp.concatenate([stack[24:32], stack[16:24, 64:96]], axis=1)
    return queries, fresh[:, :HD], fresh[:, HD:], starts, lengths


def fetch(sources, targets, sems):
    copies = [
        pltpu.make_async_copy(s, t, sems.at[i]) for i, (s, t) in enumerate(zip(sources, targets))
    ]
    for copy in copies:
        copy.start()
    return copies


def send_kernel(
    tokens, offsets_hbm, lengths_hbm, queries_hbm, fresh_hbm, out_ref, placed_ref, mine_ref,
    offsets_ref, lengths_ref, queries_ref, fresh_ref, sems,
):
    sources = (offsets_hbm, lengths_hbm, queries_hbm, fresh_hbm)
    for copy in fetch(sources, (offsets_ref, lengths_ref, queries_ref, fresh_ref), sems):
        copy.wait()
    index = lax.axis_index("req")
    rows = out_ref.shape[0]
    offsets = own_row(offsets_ref, index, 0)
    owners = offsets // tokens
    starts = column(offsets - owners * tokens, 16)
    lengths = column(own_row(lengths_ref, index, 0), 16)
    far = pltpu.roll(owners, LANES - HALF, 1)
    lane = iota((1, LANES), 1)
    spread = jnp.where(lane < 8, far, 0)
    for k in (1, 2, 3):
        here = (lane >= 8 * k) & (lane < 8 * k + 8)
        spread = spread + jnp.where(here, pltpu.roll(far, 8 * k, 1), 0)
    row = iota((rows, LANES), 0)
    col = iota((rows, LANES), 1)
    hit = ((row >> 2) == jnp.broadcast_to(spread, (rows, LANES))) & ((row & 3) == (col >> 3))
    placed = jnp.where(hit, 1.0, 0.0).astype(BF)
    placed_ref[...] = placed
    queries = queries_ref[...].astype(F32)
    fresh = fresh_ref[...].astype(F32)
    mine_ref[...] = pack(queries[:8], fresh[:8], starts[:8], lengths[:8])
    stack = pack(queries[8:], fresh[8:], starts[8:], lengths[8:])
    stack = jnp.concatenate([stack, jnp.zeros((96, LANES), F32)], axis=0)
    out_ref[...] = dot(placed, stack.astype(BF)).astype(BF)


def attend(stack, long_start, cache_ref, long_ref):
    tokens = cache_ref.shape[1]
    scale = HD ** (-0.5)
    queries, fresh_key, fresh_value, starts, lengths = unpack(stack)
    heads = [queries[:, g * HD : (g + 1) * HD] for g in range(G)]
    own = [jnp.sum(h * fresh_key, axis=1, keepdims=True) * scale for h in heads]
    is_long = lengths == LMAX

    @pl.when(jnp.max(lengths) == LMAX)
    def _():
        sub = iota((8, HD), 0)
        long_query = jnp.zeros((8, HD), F32)
        long_own = jnp.zeros((8, 1), F32)
        for g in range(G):
            picked = jnp.sum(jnp.where(is_long, heads[g], 0.0), axis=0, keepdims=True)
            long_query = jnp.where(sub == g, picked, long_query)
            picked_own = jnp.sum(jnp.where(is_long, own[g], 0.0), axis=0, keepdims=True)
            long_own = jnp.where(iota((8, 1), 0) == g, picked_own, long_own)
        long_value = jnp.sum(jnp.where(is_long, fresh_value, 0.0), axis=0, keepdims=True)
        span = W + LANES
        first = long_start + (LMAX - W + 1)
        base = jnp.minimum(first // LANES * LANES, tokens - span)
        window = pl.ds(pl.multiple_of(base, LANES), span)
        scores = dot(long_query.astype(BF), cache_ref[:HD, window]) * scale
        position = base + iota((8, span), 1)
        scores = jnp.where((position >= first) & (position < first + (W - 1)), scores, -jnp.inf)
        highest = jnp.maximum(jnp.max(scores, axis=1, keepdims=True), long_own)
        weights = jnp.exp(scores - highest)
        own_weight = jnp.exp(long_own - highest)
        totals = jnp.sum(weights, axis=1, keepdims=True) + own_weight
        summed = dot_t(weights.astype(BF), cache_ref[HD : 2 * HD, window])
        summed = summed + own_weight.astype(BF).astype(F32) * long_value
        long_ref[...] = summed / totals

    blocks = (tokens - LMAX) // LANES + 1
    before = (long_start + LANES - 1) // LANES
    after = (long_start + LMAX) // LANES
    last = tokens // LANES - 1
    keys, values, places = [], [], []
    for i in range(blocks):
        block = jnp.where(i < before, i, after + i - before)
        spare = block > last
        begin = pl.multiple_of(jnp.minimum(block, last) * LANES, LANES)
        keys.append(cache_ref[:HD, pl.ds(begin, LANES)])
        values.append(cache_ref[HD : 2 * HD, pl.ds(begin, LANES)])
        places.append(jnp.where(spare, -LANES, begin) + iota((1, LANES), 1))
    keys = jnp.concatenate(keys, axis=1)
    values = jnp.concatenate(values, axis=1)
    position = jnp.concatenate(places, axis=1)
    ends = starts + lengths
    firsts = jnp.maximum(starts, ends - (W - 1))
    ends = jnp.concatenate([ends] * G, axis=0)
    firsts = jnp.concatenate([firsts] * G, axis=0)
    own_all = jnp.concatenate(own, axis=0)
    scores = dot(jnp.concatenate(heads, axis=0).astype(BF), keys) * scale
    scores = jnp.where((position >= firsts) & (position < ends), scores, -jnp.inf)
    highest = jnp.maximum(jnp.max(scores, axis=1, keepdims=True), own_all)
    weights = jnp.exp(scores - highest)
    own_weight = jnp.exp(own_all - highest)
    totals = jnp.sum(weights, axis=1, keepdims=True) + own_weight
    summed = dot_t(weights.astype(BF), values)
    summed = summed + own_weight.astype(BF).astype(F32) * jnp.concatenate([fresh_value] * G, axis=0)
    outs = summed / totals
    long_out = long_ref[...]
    return jnp.concatenate(
        [jnp.where(is_long, long_out[g : g + 1], outs[g * 8 : g * 8 + 8]) for g in range(G)], axis=1
    )


def home_kernel(
    mine_ref, offsets_hbm, lengths_hbm, cache_hbm,
    cache_ref, home_ref, chosen_ref, long_start_ref, offsets_ref, lengths_ref, long_ref, sems,
):
    index = lax.axis_index("req")
    tokens = cache_ref.shape[1]
    sources = (offsets_hbm, lengths_hbm, cache_hbm)
    copies = fetch(sources, (offsets_ref, lengths_ref, cache_ref), sems)
    copies[0].wait()
    copies[1].wait()
    offsets = offsets_ref[...]
    held = (offsets // tokens) == index
    long_start = jnp.sum(jnp.where(held & (lengths_ref[...] == LMAX), offsets, 0)) - index * tokens
    long_start_ref[...] = jnp.full((8, LANES), long_start, I32)
    rows = chosen_ref.shape[0]
    lane = iota((8, LANES), 1)
    flags = jnp.where(held & ((lane & 15) >= HALF), 1.0, 0.0).astype(BF)
    line = iota((rows, 8), 0) >> 5
    here = dot(jnp.where(line == iota((rows, 8), 1), 1.0, 0.0).astype(BF), flags)
    earlier = dot(jnp.where(line > iota((rows, 8), 1), 1.0, 0.0).astype(BF), flags)
    row = iota((rows, LANES), 0)
    col = iota((rows, LANES), 1)
    slot = (row >> 2) & 7
    valid = jnp.sum(jnp.where((col >> 4) == slot, here, 0.0), axis=1, keepdims=True)
    rank = jnp.sum(earlier + jnp.where((col >> 4) < slot, here, 0.0), axis=1, keepdims=True)
    hit = (valid > 0.5) & (rank.astype(I32) == (col & 7)) & ((row & 3) == (col >> 3))
    chosen_ref[...] = jnp.where(hit, 1.0, 0.0).astype(BF)
    long_ref[...] = jnp.zeros_like(long_ref)
    copies[2].wait()
    home_ref[...] = attend(mine_ref[...], long_start, cache_ref, long_ref)


def far_kernel(
    got_ref, chosen_ref, long_start_ref, home_ref, cache_ref, weight_hbm, out_ref,
    weight_ref, long_ref, sems,
):
    (copy,) = fetch((weight_hbm,), (weight_ref,), sems)
    long_ref[...] = jnp.zeros_like(long_ref)
    held = dot(jnp.transpose(chosen_ref[...].astype(F32)).astype(BF), got_ref[...])
    far = attend(held[:32], jnp.max(long_start_ref[0:1, :]), cache_ref, long_ref)
    attended = jnp.concatenate([home_ref[...], far], axis=0).astype(BF)
    copy.wait()
    width = G * HD
    for j in range(out_ref.shape[0]):
        left = j * width // LANES * LANES
        out_ref[j] = dot(attended, weight_ref[:, left : left + out_ref.shape[2]]).astype(BF)


def spread_kernel(shares_ref, chosen_ref, home_ref, out_ref):
    odd = (lax.axis_index("tp") % 2) == 1
    total = jnp.sum(shares_ref[...].astype(F32), axis=0)
    moved = jnp.concatenate([total[:, 64:], total[:, :64]], axis=1)
    mixed = jnp.where(odd, moved, total).astype(BF).astype(F32)
    home_ref[...] = mixed[:8, : home_ref.shape[1]]
    far = mixed[8:]
    stack = jnp.concatenate(
        [far[:, :128], far[:, 128:256], far[:, 256:], jnp.zeros((104, LANES), F32)], axis=0
    )
    out_ref[...] = dot(chosen_ref[...], stack.astype(BF)).astype(BF)


def pick_kernel(placed_ref, home_ref, returned_ref, out_ref):
    far = dot(jnp.transpose(placed_ref[...].astype(F32)).astype(BF), returned_ref[...])
    far = jnp.concatenate([far[0:8], far[8:16], far[16:24, :64]], axis=1)
    out_ref[...] = jnp.concatenate([home_ref[...], far], axis=0).astype(BF)


def near(x):
    return pltpu.with_memory_space_constraint(x, pltpu.VMEM)


def held_back(x):
    return pltpu.with_memory_space_constraint(x, pltpu.HBM)


def call(kernel, out_shape, *args, far_args=(), scratch=(), in_hbm=False):
    outs = out_shape if in_hbm else [pltpu.VMEM(s.shape, s.dtype) for s in out_shape]
    return pl.pallas_call(
        kernel,
        out_shape=outs,
        in_specs=[NEAR] * len(args) + [ANYWHERE] * len(far_args),
        out_specs=[NEAR] * len(out_shape),
        scratch_shapes=scratch,
        compiler_params=pltpu.CompilerParams(vmem_limit_bytes=16 << 20),
    )(*(near(a) for a in args), *(held_back(a) for a in far_args))


def shards(queries, fresh_kv, kv_cache, out_weight, offsets, lengths):
    devices = lax.axis_size("req")
    columns = lax.axis_size("tp")
    row_count, width = queries.shape
    tokens = kv_cache.shape[2]
    cache = kv_cache.reshape(kv_cache.shape[1:])
    offsets = offsets.reshape(-1, LANES)
    lengths = lengths.reshape(-1, LANES)
    shape = jax.ShapeDtypeStruct
    slots = shape((devices * 4, LANES), BF)
    scratch = lambda x: pltpu.VMEM(x.shape, x.dtype)
    semaphores = pltpu.SemaphoreType.DMA
    long_scratch = pltpu.VMEM((8, HD), F32)
    inputs = (offsets, lengths, queries, fresh_kv)
    message, placed, mine = call(
        functools.partial(send_kernel, tokens),
        [slots, slots, shape((32, LANES), F32)],
        far_args=inputs,
        scratch=[*map(scratch, inputs), semaphores((4,))],
    )
    got = lax.all_to_all(message.reshape(devices, 4, LANES), "req", 0, 0, tiled=True)
    home_cache, home_out, chosen, long_start = call(
        home_kernel,
        [shape(cache.shape, BF), shape((HALF, width), F32), slots, shape((8, LANES), I32)],
        mine,
        far_args=(offsets, lengths, cache),
        scratch=[scratch(offsets), scratch(lengths), long_scratch, semaphores((3,))],
    )
    (shares,) = call(
        far_kernel,
        [shape((columns, row_count, 384), BF)],
        got.reshape(devices * 4, LANES), chosen, long_start, home_out, home_cache,
        far_args=(out_weight,),
        scratch=[scratch(out_weight), long_scratch, semaphores((1,))],
    )
    shares = lax.all_to_all(shares, "tp", 0, 0, tiled=True)
    home, spread = call(spread_kernel, [shape((HALF, width), F32), slots], shares, chosen)
    returned = lax.all_to_all(spread.reshape(devices, 4, LANES), "req", 0, 0, tiled=True)
    (mixed,) = call(
        pick_kernel,
        [shape((row_count, width), BF)],
        placed, home, returned.reshape(devices * 4, LANES),
        in_hbm=True,
    )
    return mixed


def solution(mesh):
    in_specs = (P("req", "tp"), P("req", "tp"), P("tp", None, "req"), P("tp", None), P(), P())
    out_specs = P("req", "tp")
    return jax.shard_map(shards, mesh=mesh, in_specs=in_specs, out_specs=out_specs, check_vma=False)
```

time: 67.4 us -> 60.1 us (0.89)
  blocking collectives: 56.3 us -> 30.2 us
  starting transfers between devices: 0 us -> 14.8 us
  waiting for transfers between devices: 0 us -> 6.11 us
  Pallas kernels: 10.7 us -> 8.65 us
    all_to_all x1 -> x0, blocking collectives: 25 us -> none  [shards(): lax.all_to_all(message.reshape(devices, 4, LANES), 'req', 0, 0, tiled=True)]
    all_to_all x0 -> x1, starting transfers between devices: none -> 14.8 us  [shards(): lax.all_to_all(message.reshape(devices, 4, LANES), 'req', 0, 0, tiled=True)]
    all_to_all x0 -> x1, waiting for transfers between devices: none -> 6.11 us  [shards(): lax.all_to_all(message.reshape(devices, 4, LANES), 'req', 0, 0, tiled=True)]
    pallas_call x4 -> x5, Pallas kernels: 10.7 us -> 8.65 us  [call(): pl.pallas_call(kernel, out_shape=outs, in_specs=[NEAR] * len(args) + [ANY...]
    all_to_all x1, blocking collectives: 16.9 us -> 16 us  [shards(): lax.all_to_all(spread.reshape(devices, 4, LANES), 'req', 0, 0, tiled=True)]
  transfers between devices with their start and end apart: 0 -> 1, of which waited for: 0 -> 1; matrix products, arithmetic and copies ran while one was open for 0% -> 0% of each run, Pallas kernels for 0% -> 7%
where the time goes in v3:
time: 60.1 us; the launch traced here: 59.8 us
  blocking collectives  30.2 us (50%)
  starting transfers between devices  14.8 us (25%)
  Pallas kernels  8.65 us (14%)
  waiting for transfers between devices  6.11 us (10%)
    all_to_all x1, blocking collectives, shards(): lax.all_to_all(spread.reshape(devices, 4, LANES), 'req', 0, 0, tiled=True)  16 us
    all_to_all x1, starting transfers between devices, shards(): lax.all_to_all(message.reshape(devices, 4, LANES), 'req', 0, 0, tiled=True)  14.8 us
    all_to_all x1, blocking collectives, shards(): shares = lax.all_to_all(shares, 'tp', 0, 0, tiled=True)  14.2 us
    pallas_call x5, Pallas kernels, call(): pl.pallas_call(kernel, out_shape=outs, in_specs=[NEAR] * len(args) + [ANY...  8.65 us
    all_to_all x1, waiting for transfers between devices, shards(): lax.all_to_all(message.reshape(devices, 4, LANES), 'req', 0, 0, tiled=True)  6.11 us
  transfers between devices with their start and end apart: 1, of which 1 were waited for; matrix products, arithmetic and copies ran while one was open for 0% of the time, Pallas kernels for 7%

profile of v3, /device:TPU:1, one launch (start us, length us, event | category | flops | bytes accessed | tf_op | source)
XLA Modules:
  0.0 59.8 jit_solution(11596984434479245924)
XLA Ops:
  0.0 1.8 %shard_map.64 = (bf16[256,128]{1,0:T(8,128)(2,1)}, bf16[256,128]{1,0:T(8,128)(2,1)S(1)}, f32[32,128]{1,0:T(8,128)S(1)}) custom-call(s32[8,128]{1,0:T(8,128)} %bitcast.11, s32[8,128]{1,0:T(8,128)} %bitcast.13, bf16[16,320]{1,0:T(8,128)(2,1)} %queries_hbm.1, bf16[16,160]{1,0:T(8,128)(2,1)} %fresh_hbm.1), custom_call_target="tpu_custom_call" | custom-call | tf_op jit(solution)/shard_map/pallas_call | solution.py:257
  1.8 14.8 %all-to-all-start = ((bf16[64,4,128]{2,1,0:T(4,128)(2,1)}), bf16[64,4,128]{2,1,0:T(4,128)(2,1)S(1)}, u32[]{:S(2)}, u32[]{:S(2)}) async-start(bf16[64,4,128]{2,1,0:T(4,128)(2,1)} %bitcast.2), calls=%async_computation | async-start | bytes 131072 | tf_op jit(solution)/shard_map/all_to_all | solution.py:287
  16.6 4.0 %shard_map.65 = (bf16[160,10240]{1,0:T(8,128)(2,1)S(1)}, f32[8,320]{1,0:T(8,128)S(1)}, bf16[256,128]{1,0:T(8,128)(2,1)S(1)}, s32[8,128]{1,0:T(8,128)S(1)}) custom-call(f32[32,128]{1,0:T(8,128)S(1)} %get-tuple-element.16.mine_ref, s32[8,128]{1,0:T(8,128)} %bitcast.12, s32[8,128]{1,0:T(8,128)} %bitcast.14, bf16[160,10240]{1,0:T(8,128)(2,1)} %bitcast.10), custom_call_target="tpu_custom_call" | custom-call | tf_op jit(solution)/shard_map/pallas_call | solution.py:257
  20.6 6.1 %all-to-all-done = bf16[64,4,128]{2,1,0:T(4,128)(2,1)S(1)} async-done(((bf16[64,4,128]{2,1,0:T(4,128)(2,1)}), bf16[64,4,128]{2,1,0:T(4,128)(2,1)S(1)}, u32[]{:S(2)}, u32[]{:S(2)}) %all-to-all-start) | async-done | bytes 65568 | tf_op jit(solution)/shard_map/all_to_all | solution.py:287
  26.7 1.9 %shard_map.66 = bf16[8,16,384]{2,1,0:T(8,128)(2,1)S(1)} custom-call(bf16[256,128]{1,0:T(8,128)(2,1)S(1)} %bitcast.7, bf16[256,128]{1,0:T(8,128)(2,1)S(1)} %get-tuple-element.17.chosen_ref, s32[8,128]{1,0:T(8,128)S(1)} %get-tuple-element.18.long_start_ref, f32[8,320]{1,0:T(8,128)S(1)} %get-tuple-element.19.home_ref, ...), custom_call_target="tpu_custom_call" | custom-call | tf_op jit(solution)/shard_map/pallas_call | solution.py:257
  28.6 14.2 %all_to_all.15.shares_ref = bf16[8,16,384]{2,1,0:T(8,128)(2,1)S(1)} all-to-all(bf16[8,16,384]{2,1,0:T(8,128)(2,1)S(1)} %shard_map.66), channel_id=1, replica_groups=mesh['req'=64,'tp'=8] {'tp'}, dimensions={0} | all-to-all | bytes 196608 | tf_op jit(solution)/shard_map/all_to_all | solution.py:302
  42.8 0.2 shard_map.67
  43.0 16.0 %all_to_all.16 = bf16[64,4,128]{2,1,0:T(4,128)(2,1)S(1)} all-to-all(bf16[64,4,128]{2,1,0:T(4,128)(2,1)S(1)} %bitcast.9), channel_id=1, replica_groups=mesh['req'=64,'tp'=8] {'req'}, dimensions={0} | all-to-all | bytes 131072 | tf_op jit(solution)/shard_map/all_to_all | solution.py:304
  59.0 0.8 %shard_map.68 = bf16[16,320]{1,0:T(8,128)(2,1)} custom-call(bf16[256,128]{1,0:T(8,128)(2,1)S(1)} %get-tuple-element.14.placed_ref, f32[8,320]{1,0:T(8,128)S(1)} %get-tuple-element.21.home_ref, bf16[256,128]{1,0:T(8,128)(2,1)S(1)} %bitcast.8), custom_call_target="tpu_custom_call" | custom-call | tf_op jit(solution)/shard_map/pallas_call | solution.py:257
Async XLA Ops:
  1.8 24.9 %all-to-all-start = ((bf16[64,4,128]{2,1,0:T(4,128)(2,1)}), bf16[64,4,128]{2,1,0:T(4,128)(2,1)S(1)}, u32[]{:S(2)}, u32[]{:S(2)}) async-start(bf16[64,4,128]{2,1,0:T(4,128)(2,1)} %bitcast.2), calls=%async_computation | async-start | bytes 131072 | tf_op jit(solution)/shard_map/all_to_all | solution.py:287

commit v4 on v3

--- a/solution.py
+++ b/solution.py
@@ -13,6 +13,8 @@
 LMAX = 8192
 LANES = 128
 HALF = 8
+REQ_FIRST = 52
+TP_FIRST = 4
 BF = jnp.bfloat16
 F32 = jnp.float32
 I32 = jnp.int32
@@ -89,7 +91,8 @@
     owners = offsets // tokens
     starts = column(offsets - owners * tokens, 16)
     lengths = column(own_row(lengths_ref, index, 0), 16)
-    far = pltpu.roll(owners, LANES - HALF, 1)
+    slot_of = jnp.where(owners < REQ_FIRST, owners + (rows // 4 - REQ_FIRST), owners - REQ_FIRST)
+    far = pltpu.roll(slot_of, LANES - HALF, 1)
     lane = iota((1, LANES), 1)
     spread = jnp.where(lane < 8, far, 0)
     for k in (1, 2, 3):
@@ -194,12 +197,15 @@
     rows = chosen_ref.shape[0]
     lane = iota((8, LANES), 1)
     flags = jnp.where(held & ((lane & 15) >= HALF), 1.0, 0.0).astype(BF)
-    line = iota((rows, 8), 0) >> 5
+    slots = rows // 4
+    source = (iota((rows, 8), 0) >> 2) + REQ_FIRST
+    line = jnp.where(source < slots, source, source - slots) >> 3
     here = dot(jnp.where(line == iota((rows, 8), 1), 1.0, 0.0).astype(BF), flags)
     earlier = dot(jnp.where(line > iota((rows, 8), 1), 1.0, 0.0).astype(BF), flags)
     row = iota((rows, LANES), 0)
     col = iota((rows, LANES), 1)
-    slot = (row >> 2) & 7
+    source = (row >> 2) + REQ_FIRST
+    slot = jnp.where(source < slots, source, source - slots) & 7
     valid = jnp.sum(jnp.where((col >> 4) == slot, here, 0.0), axis=1, keepdims=True)
     rank = jnp.sum(earlier + jnp.where((col >> 4) < slot, here, 0.0), axis=1, keepdims=True)
     hit = (valid > 0.5) & (rank.astype(I32) == (col & 7)) & ((row & 3) == (col >> 3))
@@ -222,7 +228,7 @@
     width = G * HD
     for j in range(out_ref.shape[0]):
         left = j * width // LANES * LANES
-        out_ref[j] = dot(attended, weight_ref[:, left : left + out_ref.shape[2]]).astype(BF)
+        out_ref[(j - TP_FIRST) % out_ref.shape[0]] = dot(attended, weight_ref[:, left : left + out_ref.shape[2]]).astype(BF)
 
 
 def spread_kernel(shares_ref, chosen_ref, home_ref, out_ref):
@@ -242,6 +248,12 @@
     far = dot(jnp.transpose(placed_ref[...].astype(F32)).astype(BF), returned_ref[...])
     far = jnp.concatenate([far[0:8], far[8:16], far[16:24, :64]], axis=1)
     out_ref[...] = jnp.concatenate([home_ref[...], far], axis=0).astype(BF)
+
+
+def exchange(x, axis, first):
+    size = lax.axis_size(axis)
+    group = [(first + i) % size for i in range(size)]
+    return lax.all_to_all(x, axis, 0, 0, axis_index_groups=[group], tiled=True)
 
 
 def near(x):
@@ -284,7 +296,7 @@
         far_args=inputs,
         scratch=[*map(scratch, inputs), semaphores((4,))],
     )
-    got = lax.all_to_all(message.reshape(devices, 4, LANES), "req", 0, 0, tiled=True)
+    got = exchange(message.reshape(devices, 4, LANES), "req", REQ_FIRST)
     home_cache, home_out, chosen, long_start = call(
         home_kernel,
         [shape(cache.shape, BF), shape((HALF, width), F32), slots, shape((8, LANES), I32)],
@@ -299,9 +311,9 @@
         far_args=(out_weight,),
         scratch=[scratch(out_weight), long_scratch, semaphores((1,))],
     )
-    shares = lax.all_to_all(shares, "tp", 0, 0, tiled=True)
+    shares = exchange(shares, "tp", TP_FIRST)
     home, spread = call(spread_kernel, [shape((HALF, width), F32), slots], shares, chosen)
-    returned = lax.all_to_all(spread.reshape(devices, 4, LANES), "req", 0, 0, tiled=True)
+    returned = exchange(spread.reshape(devices, 4, LANES), "req", REQ_FIRST)
     (mixed,) = call(
         pick_kernel,
         [shape((row_count, width), BF)],

time: 60.1 us -> 52.3 us (0.87)
  blocking collectives: 30.2 us -> 25.2 us
  waiting for transfers between devices: 6.11 us -> 1.57 us
  starting transfers between devices: 14.8 us -> 16.7 us
    all_to_all x2, blocking collectives: 30.2 us -> 25.2 us  [exchange(): return lax.all_to_all(x, axis, 0, 0, axis_index_groups=[group], tiled=True)]
    all_to_all x1, waiting for transfers between devices: 6.11 us -> 1.57 us  [exchange(): return lax.all_to_all(x, axis, 0, 0, axis_index_groups=[group], tiled=True)]
    all_to_all x1, starting transfers between devices: 14.8 us -> 16.7 us  [exchange(): return lax.all_to_all(x, axis, 0, 0, axis_index_groups=[group], tiled=True)]
  transfers between devices with their start and end apart: 1 -> 1, of which waited for: 1 -> 1; matrix products, arithmetic and copies ran while one was open for 0% -> 0% of each run, Pallas kernels for 7% -> 6%
where the time goes in v4:
time: 52.3 us; the launch traced here: 52 us
  blocking collectives  25.2 us (48%)
  starting transfers between devices  16.7 us (32%)
  Pallas kernels  8.46 us (16%)
  waiting for transfers between devices  1.57 us (3%)
    all_to_all x2, blocking collectives, exchange(): return lax.all_to_all(x, axis, 0, 0, axis_index_groups=[group], tiled=True)  25.2 us
    all_to_all x1, starting transfers between devices, exchange(): return lax.all_to_all(x, axis, 0, 0, axis_index_groups=[group], tiled=True)  16.7 us
    pallas_call x5, Pallas kernels, call(): pl.pallas_call(kernel, out_shape=outs, in_specs=[NEAR] * len(args) + [ANY...  8.46 us
    all_to_all x1, waiting for transfers between devices, exchange(): return lax.all_to_all(x, axis, 0, 0, axis_index_groups=[group], tiled=True)  1.57 us
  transfers between devices with their start and end apart: 1, of which 1 were waited for; matrix products, arithmetic and copies ran while one was open for 0% of the time, Pallas kernels for 6%

profile of v4, /device:TPU:1, one launch (start us, length us, event | category | flops | bytes accessed | tf_op | source)
XLA Modules:
  0.0 52.0 jit_solution(15999565641088989984)
XLA Ops:
  0.0 1.8 %shard_map.64 = (bf16[256,128]{1,0:T(8,128)(2,1)}, bf16[256,128]{1,0:T(8,128)(2,1)S(1)}, f32[32,128]{1,0:T(8,128)S(1)}) custom-call(s32[8,128]{1,0:T(8,128)} %bitcast.11, s32[8,128]{1,0:T(8,128)} %bitcast.13, bf16[16,320]{1,0:T(8,128)(2,1)} %queries_hbm.1, bf16[16,160]{1,0:T(8,128)(2,1)} %fresh_hbm.1), custom_call_target="tpu_custom_call" | custom-call | tf_op jit(solution)/shard_map/pallas_call | solution.py:269
  1.8 16.7 %all-to-all-start = ((bf16[64,4,128]{2,1,0:T(4,128)(2,1)}), bf16[64,4,128]{2,1,0:T(4,128)(2,1)S(1)}, u32[]{:S(2)}, u32[]{:S(2)}) async-start(bf16[64,4,128]{2,1,0:T(4,128)(2,1)} %bitcast.2), calls=%async_computation | async-start | bytes 131072 | tf_op jit(solution)/shard_map/all_to_all | solution.py:256
  18.5 3.0 %shard_map.65 = (bf16[160,10240]{1,0:T(8,128)(2,1)S(1)}, f32[8,320]{1,0:T(8,128)S(1)}, bf16[256,128]{1,0:T(8,128)(2,1)S(1)}, s32[8,128]{1,0:T(8,128)S(1)}) custom-call(f32[32,128]{1,0:T(8,128)S(1)} %get-tuple-element.16.mine_ref, s32[8,128]{1,0:T(8,128)} %bitcast.12, s32[8,128]{1,0:T(8,128)} %bitcast.14, bf16[160,10240]{1,0:T(8,128)(2,1)} %bitcast.10), custom_call_target="tpu_custom_call" | custom-call | tf_op jit(solution)/shard_map/pallas_call | solution.py:269
  21.5 1.6 %all-to-all-done = bf16[64,4,128]{2,1,0:T(4,128)(2,1)S(1)} async-done(((bf16[64,4,128]{2,1,0:T(4,128)(2,1)}), bf16[64,4,128]{2,1,0:T(4,128)(2,1)S(1)}, u32[]{:S(2)}, u32[]{:S(2)}) %all-to-all-start) | async-done | bytes 65568 | tf_op jit(solution)/shard_map/all_to_all | solution.py:256
  23.1 2.7 %shard_map.66 = bf16[8,16,384]{2,1,0:T(8,128)(2,1)S(1)} custom-call(bf16[256,128]{1,0:T(8,128)(2,1)S(1)} %bitcast.7, bf16[256,128]{1,0:T(8,128)(2,1)S(1)} %get-tuple-element.17.chosen_ref, s32[8,128]{1,0:T(8,128)S(1)} %get-tuple-element.18.long_start_ref, f32[8,320]{1,0:T(8,128)S(1)} %get-tuple-element.19.home_ref, ...), custom_call_target="tpu_custom_call" | custom-call | tf_op jit(solution)/shard_map/pallas_call | solution.py:269
  25.8 11.1 %all_to_all.15.shares_ref = bf16[8,16,384]{2,1,0:T(8,128)(2,1)S(1)} all-to-all(bf16[8,16,384]{2,1,0:T(8,128)(2,1)S(1)} %shard_map.66), channel_id=1, replica_groups={{4,5,6,7,0,1,2,3},{12,13,14,15,8,9,10,11},{20,21,22,23,16,17,18,19},{28..., dimensions={0} | all-to-all | bytes 196608 | tf_op jit(solution)/shard_map/all_to_all | solution.py:256
  36.9 0.2 shard_map.67
  37.1 14.1 %all_to_all.16 = bf16[64,4,128]{2,1,0:T(4,128)(2,1)S(1)} all-to-all(bf16[64,4,128]{2,1,0:T(4,128)(2,1)S(1)} %bitcast.9), channel_id=1, replica_groups={{416,424,432,440,448,456,464,472,480,488,496,504,0,8,16,24,32,40,48,56,..., dimensions={0} | all-to-all | bytes 131072 | tf_op jit(solution)/shard_map/all_to_all | solution.py:256
  51.2 0.8 %shard_map.68 = bf16[16,320]{1,0:T(8,128)(2,1)} custom-call(bf16[256,128]{1,0:T(8,128)(2,1)S(1)} %get-tuple-element.14.placed_ref, f32[8,320]{1,0:T(8,128)S(1)} %get-tuple-element.21.home_ref, bf16[256,128]{1,0:T(8,128)(2,1)S(1)} %bitcast.8), custom_call_target="tpu_custom_call" | custom-call | tf_op jit(solution)/shard_map/pallas_call | solution.py:269
Async XLA Ops:
  1.8 21.3 %all-to-all-start = ((bf16[64,4,128]{2,1,0:T(4,128)(2,1)}), bf16[64,4,128]{2,1,0:T(4,128)(2,1)S(1)}, u32[]{:S(2)}, u32[]{:S(2)}) async-start(bf16[64,4,128]{2,1,0:T(4,128)(2,1)} %bitcast.2), calls=%async_computation | async-start | bytes 131072 | tf_op jit(solution)/shard_map/all_to_all | solution.py:256

commit v5 on v4

v5 whole, which is shorter than its diff:
```python
import functools

import jax
import jax.numpy as jnp
from jax import lax
from jax.experimental import pallas as pl
from jax.experimental.pallas import tpu as pltpu
from jax.sharding import PartitionSpec as P

HD = 80
G = 4
W = 4096
LMAX = 8192
LANES = 128
HALF = 8
REQ_FIRST = 52
TP_FIRST = 4
BF = jnp.bfloat16
F32 = jnp.float32
I32 = jnp.int32
NEAR = pl.BlockSpec(memory_space=pltpu.VMEM)
ANYWHERE = pl.BlockSpec(memory_space=pltpu.HBM)


def iota(shape, axis):
    return lax.broadcasted_iota(I32, shape, axis)


def dot(a, b):
    return jnp.dot(a, b, preferred_element_type=F32)


def dot_t(a, b):
    return lax.dot_general(a, b, (((1,), (1,)), ((), ())), preferred_element_type=F32)


def owner_of(offsets, tokens):
    return ((offsets.astype(F32) + 0.5) * (1.0 / tokens)).astype(I32)


def own_row(table_ref, index, shift):
    per_row = LANES // 16
    row = table_ref[pl.ds(index // per_row, 1), :]
    back = (index % per_row) * 16 + shift
    return pltpu.roll(row, (LANES - back) % LANES, 1)


def column(row, count):
    wide = jnp.broadcast_to(row, (count, LANES))
    same = iota((count, LANES), 0) == iota((count, LANES), 1)
    return jnp.sum(jnp.where(same, wide, 0), axis=1, keepdims=True)


def pack(queries, fresh, starts, lengths):
    lane = iota((HALF, LANES), 1)
    meta = jnp.where(lane == 96, 1, 0)
    meta = jnp.where(lane == 97, starts >> 7, meta)
    meta = jnp.where(lane == 98, starts & 127, meta)
    meta = jnp.where(lane == 99, lengths >> 7, meta)
    meta = jnp.where(lane == 100, lengths & 127, meta)
    third = jnp.concatenate([queries[:, 256:], fresh[:, 128:], jnp.zeros((HALF, 32), F32)], axis=1)
    return jnp.concatenate(
        [queries[:, :128], queries[:, 128:256], third + meta.astype(F32), fresh[:, :128]], axis=0
    )


def unpack(stack):
    meta = stack[16:24]
    starts = (meta[:, 97:98] * 128.0 + meta[:, 98:99]).astype(I32)
    lengths = (meta[:, 99:100] * 128.0 + meta[:, 100:101]).astype(I32)
    queries = jnp.concatenate([stack[0:8], stack[8:16], stack[16:24, :64]], axis=1)
    fresh = jnp.concatenate([stack[24:32], stack[16:24, 64:96]], axis=1)
    return queries, fresh[:, :HD], fresh[:, HD:], starts, lengths


def fetch(sources, targets, sems):
    copies = [
        pltpu.make_async_copy(s, t, sems.at[i]) for i, (s, t) in enumerate(zip(sources, targets))
    ]
    for copy in copies:
        copy.start()
    return copies


def slot_of(owners, slots):
    return jnp.where(owners < REQ_FIRST, owners + (slots - REQ_FIRST), owners - REQ_FIRST)


def send_kernel(
    tokens, offsets_hbm, lengths_hbm, queries_hbm, fresh_hbm, out_ref,
    offsets_ref, lengths_ref, queries_ref, fresh_ref, sems,
):
    sources = (offsets_hbm, lengths_hbm, queries_hbm, fresh_hbm)
    for copy in fetch(sources, (offsets_ref, lengths_ref, queries_ref, fresh_ref), sems):
        copy.wait()
    index = lax.axis_index("req")
    rows = out_ref.shape[0]
    offsets = own_row(offsets_ref, index, HALF)
    owners = owner_of(offsets, tokens)
    starts = column(offsets - owners * tokens, HALF)
    lengths = column(own_row(lengths_ref, index, HALF), HALF)
    far = slot_of(owners, rows // 4)
    lane = iota((1, LANES), 1)
    spread = jnp.where(lane < 8, far, 0)
    for k in (1, 2, 3):
        here = (lane >= 8 * k) & (lane < 8 * k + 8)
        spread = spread + jnp.where(here, pltpu.roll(far, 8 * k, 1), 0)
    row = iota((rows, LANES), 0)
    col = iota((rows, LANES), 1)
    hit = ((row >> 2) == jnp.broadcast_to(spread, (rows, LANES))) & ((row & 3) == (col >> 3))
    placed = jnp.where(hit, 1.0, 0.0).astype(BF)
    queries = queries_ref[...].astype(F32)
    fresh = fresh_ref[...].astype(F32)
    stack = pack(queries[8:], fresh[8:], starts, lengths)
    stack = jnp.concatenate([stack, jnp.zeros((96, LANES), F32)], axis=0)
    out_ref[...] = dot(placed, stack.astype(BF)).astype(BF)


def weigh(queries, keys, values, inside, own, own_value):
    scores = jnp.where(inside, dot(queries.astype(BF), keys) * HD ** (-0.5), -jnp.inf)
    highest = jnp.maximum(jnp.max(scores, axis=1, keepdims=True), own)
    weights = jnp.exp(scores - highest)
    own_weight = jnp.exp(own - highest)
    totals = jnp.sum(weights, axis=1, keepdims=True) + own_weight
    summed = dot_t(weights.astype(BF), values) + own_weight.astype(BF).astype(F32) * own_value
    return summed / totals


def attend(queries, fresh_key, fresh_value, starts, lengths, long_start, cache_ref):
    tokens = cache_ref.shape[1]
    heads = [queries[:, g * HD : (g + 1) * HD] for g in range(G)]
    own = [jnp.sum(h * fresh_key, axis=1, keepdims=True) * HD ** (-0.5) for h in heads]
    is_long = lengths == LMAX
    long_query = jnp.zeros((8, HD), F32)
    long_own = jnp.zeros((8, 1), F32)
    for g in range(G):
        picked = jnp.sum(jnp.where(is_long, heads[g], 0.0), axis=0, keepdims=True)
        long_query = jnp.where(iota((8, HD), 0) == g, picked, long_query)
        picked_own = jnp.sum(jnp.where(is_long, own[g], 0.0), axis=0, keepdims=True)
        long_own = jnp.where(iota((8, 1), 0) == g, picked_own, long_own)
    long_value = jnp.sum(jnp.where(is_long, fresh_value, 0.0), axis=0, keepdims=True)
    span = W + LANES
    first = long_start + (LMAX - W + 1)
    base = jnp.minimum(first // LANES * LANES, tokens - span)
    window = pl.ds(pl.multiple_of(base, LANES), span)
    position = base + iota((8, span), 1)
    long_out = weigh(
        long_query,
        cache_ref[:HD, window],
        cache_ref[HD : 2 * HD, window],
        (position >= first) & (position < first + (W - 1)),
        long_own,
        long_value,
    )
    blocks = (tokens - LMAX) // LANES + 1
    before = (long_start + LANES - 1) // LANES
    after = (long_start + LMAX) // LANES
    last = tokens // LANES - 1
    keys, values, places = [], [], []
    for i in range(blocks):
        block = jnp.where(i < before, i, after + i - before)
        spare = block > last
        begin = pl.multiple_of(jnp.minimum(block, last) * LANES, LANES)
        keys.append(cache_ref[:HD, pl.ds(begin, LANES)])
        values.append(cache_ref[HD : 2 * HD, pl.ds(begin, LANES)])
        places.append(jnp.where(spare, -LANES, begin) + iota((1, LANES), 1))
    position = jnp.concatenate(places, axis=1)
    ends = starts + lengths
    firsts = jnp.maximum(starts, ends - (W - 1))
    ends = jnp.concatenate([ends] * G, axis=0)
    firsts = jnp.concatenate([firsts] * G, axis=0)
    outs = weigh(
        jnp.concatenate(heads, axis=0),
        jnp.concatenate(keys, axis=1),
        jnp.concatenate(values, axis=1),
        (position >= firsts) & (position < ends),
        jnp.concatenate(own, axis=0),
        jnp.concatenate([fresh_value] * G, axis=0),
    )
    return jnp.concatenate(
        [jnp.where(is_long, long_out[g : g + 1], outs[g * 8 : g * 8 + 8]) for g in range(G)], axis=1
    )


def home_kernel(
    offsets_hbm, lengths_hbm, queries_hbm, fresh_hbm, cache_hbm,
    cache_ref, home_ref, chosen_ref, chosen_t_ref, placed_t_ref, long_start_ref,
    offsets_ref, lengths_ref, queries_ref, fresh_ref, sems,
):
    sources = (offsets_hbm, lengths_hbm, queries_hbm, fresh_hbm, cache_hbm)
    copies = fetch(sources, (offsets_ref, lengths_ref, queries_ref, fresh_ref, cache_ref), sems)
    for copy in copies[:4]:
        copy.wait()
    index = lax.axis_index("req")
    tokens = cache_ref.shape[1]
    rows = chosen_ref.shape[0]
    slots = rows // 4
    offsets = offsets_ref[...]
    held = owner_of(offsets, tokens) == index
    long_start = jnp.sum(jnp.where(held & (lengths_ref[...] == LMAX), offsets, 0)) - index * tokens
    long_start_ref[...] = jnp.full((8, LANES), long_start, I32)
    flags = jnp.where(held & ((iota((8, LANES), 1) & 15) >= HALF), 1.0, 0.0).astype(BF)
    source = (iota((rows, 8), 0) >> 2) + REQ_FIRST
    line = jnp.where(source < slots, source, source - slots) >> 3
    here = dot(jnp.where(line == iota((rows, 8), 1), 1.0, 0.0).astype(BF), flags)
    earlier = dot(jnp.where(line > iota((rows, 8), 1), 1.0, 0.0).astype(BF), flags)
    row = iota((rows, LANES), 0)
    col = iota((rows, LANES), 1)
    source = (row >> 2) + REQ_FIRST
    slot = jnp.where(source < slots, source, source - slots) & 7
    valid = jnp.sum(jnp.where((col >> 4) == slot, here, 0.0), axis=1, keepdims=True)
    rank = jnp.sum(earlier + jnp.where((col >> 4) < slot, here, 0.0), axis=1, keepdims=True)
    hit = (valid > 0.5) & (rank.astype(I32) == (col & 7)) & ((row & 3) == (col >> 3))
    chosen = jnp.where(hit, 1.0, 0.0)
    chosen_ref[...] = chosen.astype(BF)
    chosen_t_ref[...] = jnp.transpose(chosen)[:32].astype(BF)
    offsets = own_row(offsets_ref, index, 0)
    starts = column(offsets, 16)
    lengths = column(own_row(lengths_ref, index, 0), 16)
    far = slot_of(owner_of(starts[8:], tokens), slots)
    far = jnp.concatenate([far] * 4, axis=0)
    row = iota((32, rows), 0)
    col = iota((32, rows), 1)
    placed_t_ref[...] = jnp.where(((col >> 2) == far) & ((col & 3) == (row >> 3)), 1.0, 0.0).astype(BF)
    queries = queries_ref[...].astype(F32)[:8]
    fresh = fresh_ref[...].astype(F32)[:8]
    copies[4].wait()
    home_ref[...] = attend(
        queries, fresh[:, :HD], fresh[:, HD:], starts[:8] - index * tokens, lengths[:8],
        long_start, cache_ref,
    )


def far_kernel(
    got_ref, chosen_t_ref, long_start_ref, home_ref, cache_ref, weight_hbm, out_ref,
    weight_ref, sems,
):
    (copy,) = fetch((weight_hbm,), (weight_ref,), sems)
    held = dot(chosen_t_ref[...], got_ref[...])
    far = attend(*unpack(held), jnp.max(long_start_ref[0:1, :]), cache_ref)
    attended = jnp.concatenate([home_ref[...], far], axis=0).astype(BF)
    copy.wait()
    mixed = dot(attended, weight_ref[...])
    columns = out_ref.shape[0]
    low = iota((HALF, LANES), 1) < 64
    for j in range(columns):
        left = j * G * HD // LANES * LANES
        tiles = [mixed[:, left + k * LANES : left + (k + 1) * LANES] for k in range(3)]
        if j % 2 == 0:
            half = jnp.where(low, tiles[2][:8], pltpu.roll(tiles[2][8:], 64, 1))
            full = tiles[:2]
        else:
            half = jnp.where(low, pltpu.roll(tiles[0][:8], 64, 1), tiles[0][8:])
            full = tiles[1:]
        out_ref[(j - TP_FIRST) % columns] = jnp.concatenate([*full, half], axis=0).astype(BF)


def spread_kernel(shares_ref, chosen_ref, home_ref, out_ref):
    mixed = jnp.sum(shares_ref[...].astype(F32), axis=0).astype(BF).astype(F32)
    home_ref[...] = mixed
    stack = jnp.concatenate(
        [mixed[8:16], mixed[24:32], mixed[32:40], jnp.zeros((104, LANES), F32)], axis=0
    )
    out_ref[...] = dot(chosen_ref[...], stack.astype(BF)).astype(BF)


def pick_kernel(placed_t_ref, home_ref, returned_ref, out_ref):
    far = dot(placed_t_ref[...], returned_ref[...])
    home = home_ref[...]
    first = jnp.concatenate([home[0:8], far[0:8]], axis=0)
    second = jnp.concatenate([home[16:24], far[8:16]], axis=0)
    half = jnp.concatenate([home[32:40], pltpu.roll(far[16:24], 64, 1)], axis=0)[:, :64]
    odd = (lax.axis_index("tp") % 2) == 1
    even = jnp.concatenate([first, second, half], axis=1)
    out_ref[...] = jnp.where(odd, jnp.concatenate([half, first, second], axis=1), even).astype(BF)


def exchange(x, axis, first):
    size = lax.axis_size(axis)
    group = [(first + i) % size for i in range(size)]
    return lax.all_to_all(x, axis, 0, 0, axis_index_groups=[group], tiled=True)


def near(x):
    return pltpu.with_memory_space_constraint(x, pltpu.VMEM)


def held_back(x):
    return pltpu.with_memory_space_constraint(x, pltpu.HBM)


def call(kernel, out_shape, *args, far_args=(), scratch=(), in_hbm=False):
    outs = out_shape if in_hbm else [pltpu.VMEM(s.shape, s.dtype) for s in out_shape]
    return pl.pallas_call(
        kernel,
        out_shape=outs,
        in_specs=[NEAR] * len(args) + [ANYWHERE] * len(far_args),
        out_specs=[NEAR] * len(out_shape),
        scratch_shapes=scratch,
        compiler_params=pltpu.CompilerParams(vmem_limit_bytes=16 << 20),
    )(*(near(a) for a in args), *(held_back(a) for a in far_args))


def shards(queries, fresh_kv, kv_cache, out_weight, offsets, lengths):
    devices = lax.axis_size("req")
    columns = lax.axis_size("tp")
    row_count, width = queries.shape
    tokens = kv_cache.shape[2]
    cache = kv_cache.reshape(kv_cache.shape[1:])
    offsets = offsets.reshape(-1, LANES)
    lengths = lengths.reshape(-1, LANES)
    shape = jax.ShapeDtypeStruct
    slots = shape((devices * 4, LANES), BF)
    scratch = lambda x: pltpu.VMEM(x.shape, x.dtype)
    semaphores = pltpu.SemaphoreType.DMA
    inputs = (offsets, lengths, queries, fresh_kv)
    (message,) = call(
        functools.partial(send_kernel, tokens),
        [slots],
        far_args=inputs,
        scratch=[*map(scratch, inputs), semaphores((4,))],
    )
    got = exchange(message.reshape(devices, 4, LANES), "req", REQ_FIRST)
    home_cache, home_out, chosen, chosen_t, placed_t, long_start = call(
        home_kernel,
        [
            shape(cache.shape, BF),
            shape((HALF, width), F32),
            slots,
            shape((32, devices * 4), BF),
            shape((32, devices * 4), BF),
            shape((8, LANES), I32),
        ],
        far_args=(*inputs, cache),
        scratch=[*map(scratch, inputs), semaphores((5,))],
    )
    (shares,) = call(
        far_kernel,
        [shape((columns, 40, LANES), BF)],
        got.reshape(devices * 4, LANES), chosen_t, long_start, home_out, home_cache,
        far_args=(out_weight,),
        scratch=[scratch(out_weight), semaphores((1,))],
    )
    shares = exchange(shares, "tp", TP_FIRST)
    home, spread = call(spread_kernel, [shape((40, LANES), F32), slots], shares, chosen)
    returned = exchange(spread.reshape(devices, 4, LANES), "req", REQ_FIRST)
    (mixed,) = call(
        pick_kernel,
        [shape((row_count, width), BF)],
        placed_t, home, returned.reshape(devices * 4, LANES),
        in_hbm=True,
    )
    return mixed


def solution(mesh):
    in_specs = (P("req", "tp"), P("req", "tp"), P("tp", None, "req"), P("tp", None), P(), P())
    out_specs = P("req", "tp")
    return jax.shard_map(shards, mesh=mesh, in_specs=in_specs, out_specs=out_specs, check_vma=False)
```

time: 52.3 us -> 51.8 us (level)
  no operation moved by 1% of the time
where the time goes in v5:
time: 51.8 us; the launch traced here: 51.5 us
  blocking collectives  24.8 us (48%)
  starting transfers between devices  16.7 us (32%)
  Pallas kernels  8.53 us (16%)
  waiting for transfers between devices  1.36 us (3%)
    all_to_all x2, blocking collectives, exchange(): return lax.all_to_all(x, axis, 0, 0, axis_index_groups=[group], tiled=True)  24.8 us
    all_to_all x1, starting transfers between devices, exchange(): return lax.all_to_all(x, axis, 0, 0, axis_index_groups=[group], tiled=True)  16.7 us
    pallas_call x5, Pallas kernels, call(): pl.pallas_call(kernel, out_shape=outs, in_specs=[NEAR] * len(args) + [ANY...  8.53 us
    all_to_all x1, waiting for transfers between devices, exchange(): return lax.all_to_all(x, axis, 0, 0, axis_index_groups=[group], tiled=True)  1.36 us
  transfers between devices with their start and end apart: 1, of which 1 were waited for; matrix products, arithmetic and copies ran while one was open for 0% of the time, Pallas kernels for 6%

profile of v5, /device:TPU:1, one launch (start us, length us, event | category | flops | bytes accessed | tf_op | source)
XLA Modules:
  0.0 51.5 jit_solution(6299783618737302727)
XLA Ops:
  0.0 1.7 %shard_map.65 = bf16[256,128]{1,0:T(8,128)(2,1)} custom-call(s32[8,128]{1,0:T(8,128)} %bitcast.11, s32[8,128]{1,0:T(8,128)} %bitcast.13, bf16[16,320]{1,0:T(8,128)(2,1)} %queries_hbm.3, bf16[16,160]{1,0:T(8,128)(2,1)} %fresh_hbm.3), custom_call_target="tpu_custom_call" | custom-call | tf_op jit(solution)/shard_map/pallas_call | solution.py:294
  1.7 16.7 %all-to-all-start = ((bf16[64,4,128]{2,1,0:T(4,128)(2,1)}), bf16[64,4,128]{2,1,0:T(4,128)(2,1)S(1)}, u32[]{:S(2)}, u32[]{:S(2)}) async-start(bf16[64,4,128]{2,1,0:T(4,128)(2,1)} %bitcast.3), calls=%async_computation | async-start | bytes 131072 | tf_op jit(solution)/shard_map/all_to_all | solution.py:281
  18.5 3.2 %shard_map.64 = (bf16[160,10240]{1,0:T(8,128)(2,1)S(1)}, f32[8,320]{1,0:T(8,128)S(1)}, bf16[256,128]{1,0:T(8,128)(2,1)S(1)}, bf16[32,256]{1,0:T(8,128)(2,1)S(1)}...) custom-call(s32[8,128]{1,0:T(8,128)} %bitcast.12, s32[8,128]{1,0:T(8,128)} %bitcast.14, bf16[16,320]{1,0:T(8,128)(2,1)} %queries_hbm.3, ...), custom_call_target="tpu_custom_call" | custom-call | tf_op jit(solution)/shard_map/pallas_call | solution.py:294
  21.7 1.4 %all-to-all-done = bf16[64,4,128]{2,1,0:T(4,128)(2,1)S(1)} async-done(((bf16[64,4,128]{2,1,0:T(4,128)(2,1)}), bf16[64,4,128]{2,1,0:T(4,128)(2,1)S(1)}, u32[]{:S(2)}, u32[]{:S(2)}) %all-to-all-start) | async-done | bytes 65568 | tf_op jit(solution)/shard_map/all_to_all | solution.py:281
  23.0 2.7 %shard_map.66 = bf16[8,40,128]{2,1,0:T(8,128)(2,1)S(1)} custom-call(bf16[256,128]{1,0:T(8,128)(2,1)S(1)} %bitcast.7, bf16[32,256]{1,0:T(8,128)(2,1)S(1)} %get-tuple-element.14.chosen_t_ref, s32[8,128]{1,0:T(8,128)S(1)} %get-tuple-element.15.long_start_ref, f32[8,320]{1,0:T(8,128)S(1)} %get-tuple-element.16.home_ref, ...), custom_call_target="tpu_custom_call" | custom-call | tf_op jit(solution)/shard_map/pallas_call | solution.py:294
  25.7 10.6 %all_to_all.15.shares_ref = bf16[8,40,128]{2,1,0:T(8,128)(2,1)S(1)} all-to-all(bf16[8,40,128]{2,1,0:T(8,128)(2,1)S(1)} %shard_map.66), channel_id=1, replica_groups={{4,5,6,7,0,1,2,3},{12,13,14,15,8,9,10,11},{20,21,22,23,16,17,18,19},{28..., dimensions={0} | all-to-all | bytes 163840 | tf_op jit(solution)/shard_map/all_to_all | solution.py:281
  36.3 0.1 shard_map.67
  36.5 14.2 %all_to_all.16 = bf16[64,4,128]{2,1,0:T(4,128)(2,1)S(1)} all-to-all(bf16[64,4,128]{2,1,0:T(4,128)(2,1)S(1)} %bitcast.9), channel_id=1, replica_groups={{416,424,432,440,448,456,464,472,480,488,496,504,0,8,16,24,32,40,48,56,..., dimensions={0} | all-to-all | bytes 131072 | tf_op jit(solution)/shard_map/all_to_all | solution.py:281
  50.7 0.8 %shard_map.68 = bf16[16,320]{1,0:T(8,128)(2,1)} custom-call(bf16[32,256]{1,0:T(8,128)(2,1)S(1)} %get-tuple-element.13.placed_t_ref, f32[40,128]{1,0:T(8,128)S(1)} %get-tuple-element.19.home_ref, bf16[256,128]{1,0:T(8,128)(2,1)S(1)} %bitcast.8), custom_call_target="tpu_custom_call" | custom-call | tf_op jit(solution)/shard_map/pallas_call | solution.py:294
Async XLA Ops:
  1.7 21.3 %all-to-all-start = ((bf16[64,4,128]{2,1,0:T(4,128)(2,1)}), bf16[64,4,128]{2,1,0:T(4,128)(2,1)S(1)}, u32[]{:S(2)}, u32[]{:S(2)}) async-start(bf16[64,4,128]{2,1,0:T(4,128)(2,1)} %bitcast.3), calls=%async_computation | async-start | bytes 131072 | tf_op jit(solution)/shard_map/all_to_all | solution.py:281

commit v6 on v5

--- a/solution.py
+++ b/solution.py
@@ -126,8 +126,22 @@
     return summed / totals
 
 
-def attend(queries, fresh_key, fresh_value, starts, lengths, long_start, cache_ref):
-    tokens = cache_ref.shape[1]
+def places(long_start, tokens):
+    before = (long_start + LANES - 1) // LANES
+    after = (long_start + LMAX) // LANES
+    last = tokens // LANES - 1
+    blocks = []
+    for i in range((tokens - LMAX) // LANES + 1):
+        block = jnp.where(i < before, i, after + i - before)
+        blocks.append((pl.multiple_of(jnp.minimum(block, last) * LANES, LANES), block > last))
+    first = long_start + (LMAX - W + 1)
+    base = jnp.minimum(first // LANES * LANES, tokens - (W + LANES))
+    return blocks, first, pl.multiple_of(base, LANES)
+
+
+def attend(queries, fresh_key, fresh_value, starts, lengths, long_start, tokens, near_ref):
+    blocks, first, base = places(long_start, tokens)
+    others, span = len(blocks) * LANES, W + LANES
     heads = [queries[:, g * HD : (g + 1) * HD] for g in range(G)]
     own = [jnp.sum(h * fresh_key, axis=1, keepdims=True) * HD ** (-0.5) for h in heads]
     is_long = lengths == LMAX
@@ -139,40 +153,26 @@
         picked_own = jnp.sum(jnp.where(is_long, own[g], 0.0), axis=0, keepdims=True)
         long_own = jnp.where(iota((8, 1), 0) == g, picked_own, long_own)
     long_value = jnp.sum(jnp.where(is_long, fresh_value, 0.0), axis=0, keepdims=True)
-    span = W + LANES
-    first = long_start + (LMAX - W + 1)
-    base = jnp.minimum(first // LANES * LANES, tokens - span)
-    window = pl.ds(pl.multiple_of(base, LANES), span)
     position = base + iota((8, span), 1)
     long_out = weigh(
         long_query,
-        cache_ref[:HD, window],
-        cache_ref[HD : 2 * HD, window],
+        near_ref[:HD, others:],
+        near_ref[HD : 2 * HD, others:],
         (position >= first) & (position < first + (W - 1)),
         long_own,
         long_value,
     )
-    blocks = (tokens - LMAX) // LANES + 1
-    before = (long_start + LANES - 1) // LANES
-    after = (long_start + LMAX) // LANES
-    last = tokens // LANES - 1
-    keys, values, places = [], [], []
-    for i in range(blocks):
-        block = jnp.where(i < before, i, after + i - before)
-        spare = block > last
-        begin = pl.multiple_of(jnp.minimum(block, last) * LANES, LANES)
-        keys.append(cache_ref[:HD, pl.ds(begin, LANES)])
-        values.append(cache_ref[HD : 2 * HD, pl.ds(begin, LANES)])
-        places.append(jnp.where(spare, -LANES, begin) + iota((1, LANES), 1))
-    position = jnp.concatenate(places, axis=1)
+    position = jnp.concatenate(
+        [jnp.where(spare, -LANES, begin) + iota((1, LANES), 1) for begin, spare in blocks], axis=1
+    )
     ends = starts + lengths
     firsts = jnp.maximum(starts, ends - (W - 1))
     ends = jnp.concatenate([ends] * G, axis=0)
     firsts = jnp.concatenate([firsts] * G, axis=0)
     outs = weigh(
         jnp.concatenate(heads, axis=0),
-        jnp.concatenate(keys, axis=1),
-        jnp.concatenate(values, axis=1),
+        near_ref[:HD, :others],
+        near_ref[HD : 2 * HD, :others],
         (position >= firsts) & (position < ends),
         jnp.concatenate(own, axis=0),
         jnp.concatenate([fresh_value] * G, axis=0),
@@ -183,21 +183,29 @@
 
 
 def home_kernel(
-    offsets_hbm, lengths_hbm, queries_hbm, fresh_hbm, cache_hbm,
-    cache_ref, home_ref, chosen_ref, chosen_t_ref, placed_t_ref, long_start_ref,
-    offsets_ref, lengths_ref, queries_ref, fresh_ref, sems,
+    offsets_hbm, lengths_hbm, queries_hbm, fresh_hbm, cache_hbm, weight_hbm,
+    near_ref, weight_ref, home_ref, chosen_ref, chosen_t_ref, placed_t_ref, long_start_ref,
+    offsets_ref, lengths_ref, queries_ref, fresh_ref, sems, weight_sems, near_sems,
 ):
-    sources = (offsets_hbm, lengths_hbm, queries_hbm, fresh_hbm, cache_hbm)
-    copies = fetch(sources, (offsets_ref, lengths_ref, queries_ref, fresh_ref, cache_ref), sems)
-    for copy in copies[:4]:
+    sources = (offsets_hbm, lengths_hbm, queries_hbm, fresh_hbm)
+    copies = fetch(sources, (offsets_ref, lengths_ref, queries_ref, fresh_ref), sems)
+    weight_rows = pl.ds(0, weight_ref.shape[0])
+    (weight_copy,) = fetch((weight_hbm.at[weight_rows],), (weight_ref,), weight_sems)
+    for copy in copies[:2]:
         copy.wait()
     index = lax.axis_index("req")
-    tokens = cache_ref.shape[1]
+    tokens = cache_hbm.shape[1]
     rows = chosen_ref.shape[0]
     slots = rows // 4
     offsets = offsets_ref[...]
     held = owner_of(offsets, tokens) == index
     long_start = jnp.sum(jnp.where(held & (lengths_ref[...] == LMAX), offsets, 0)) - index * tokens
+    blocks, _, base = places(long_start, tokens)
+    sources = [cache_hbm.at[:, pl.ds(begin, LANES)] for begin, _ in blocks]
+    targets = [near_ref.at[:, pl.ds(i * LANES, LANES)] for i in range(len(blocks))]
+    sources.append(cache_hbm.at[:, pl.ds(base, W + LANES)])
+    targets.append(near_ref.at[:, pl.ds(len(blocks) * LANES, W + LANES)])
+    near_copies = fetch(sources, targets, near_sems)
     long_start_ref[...] = jnp.full((8, LANES), long_start, I32)
     flags = jnp.where(held & ((iota((8, LANES), 1) & 15) >= HALF), 1.0, 0.0).astype(BF)
     source = (iota((rows, 8), 0) >> 2) + REQ_FIRST
@@ -222,25 +230,30 @@
     row = iota((32, rows), 0)
     col = iota((32, rows), 1)
     placed_t_ref[...] = jnp.where(((col >> 2) == far) & ((col & 3) == (row >> 3)), 1.0, 0.0).astype(BF)
+    for copy in copies[2:]:
+        copy.wait()
     queries = queries_ref[...].astype(F32)[:8]
     fresh = fresh_ref[...].astype(F32)[:8]
-    copies[4].wait()
+    for copy in near_copies:
+        copy.wait()
     home_ref[...] = attend(
         queries, fresh[:, :HD], fresh[:, HD:], starts[:8] - index * tokens, lengths[:8],
-        long_start, cache_ref,
-    )
+        long_start, tokens, near_ref,
+    )
+    weight_copy.wait()
 
 
 def far_kernel(
-    got_ref, chosen_t_ref, long_start_ref, home_ref, cache_ref, weight_hbm, out_ref,
-    weight_ref, sems,
+    tokens, got_ref, chosen_t_ref, long_start_ref, home_ref, near_ref, weight_ref, weight_hbm, out_ref,
+    rest_ref, sems,
 ):
-    (copy,) = fetch((weight_hbm,), (weight_ref,), sems)
+    upper, rest = weight_ref.shape[0], rest_ref.shape[0]
+    (copy,) = fetch((weight_hbm.at[pl.ds(upper, rest)],), (rest_ref,), sems)
     held = dot(chosen_t_ref[...], got_ref[...])
-    far = attend(*unpack(held), jnp.max(long_start_ref[0:1, :]), cache_ref)
+    far = attend(*unpack(held), jnp.max(long_start_ref[0:1, :]), tokens, near_ref)
     attended = jnp.concatenate([home_ref[...], far], axis=0).astype(BF)
     copy.wait()
-    mixed = dot(attended, weight_ref[...])
+    mixed = dot(attended[:, :upper], weight_ref[...]) + dot(attended[:, upper:], rest_ref[...])
     columns = out_ref.shape[0]
     low = iota((HALF, LANES), 1) < 64
     for j in range(columns):
@@ -321,25 +334,32 @@
         scratch=[*map(scratch, inputs), semaphores((4,))],
     )
     got = exchange(message.reshape(devices, 4, LANES), "req", REQ_FIRST)
-    home_cache, home_out, chosen, chosen_t, placed_t, long_start = call(
+    near_blocks = (tokens - LMAX) // LANES + 1
+    upper = out_weight.shape[0] * 4 // 5
+    home_near, home_weight, home_out, chosen, chosen_t, placed_t, long_start = call(
         home_kernel,
         [
-            shape(cache.shape, BF),
+            shape((2 * HD, near_blocks * LANES + W + LANES), BF),
+            shape((upper, out_weight.shape[1]), BF),
             shape((HALF, width), F32),
             slots,
             shape((32, devices * 4), BF),
             shape((32, devices * 4), BF),
             shape((8, LANES), I32),
         ],
-        far_args=(*inputs, cache),
-        scratch=[*map(scratch, inputs), semaphores((5,))],
+        far_args=(*inputs, cache, out_weight),
+        scratch=[
+            *map(scratch, inputs), semaphores((4,)), semaphores((1,)), semaphores((near_blocks + 1,))
+        ],
     )
     (shares,) = call(
-        far_kernel,
+        functools.partial(far_kernel, tokens),
         [shape((columns, 40, LANES), BF)],
-        got.reshape(devices * 4, LANES), chosen_t, long_start, home_out, home_cache,
+        got.reshape(devices * 4, LANES), chosen_t, long_start, home_out, home_near, home_weight,
         far_args=(out_weight,),
-        scratch=[scratch(out_weight), semaphores((1,))],
+        scratch=[
+            pltpu.VMEM((out_weight.shape[0] - upper, out_weight.shape[1]), BF), semaphores((1,))
+        ],
     )
     shares = exchange(shares, "tp", TP_FIRST)
     home, spread = call(spread_kernel, [shape((40, LANES), F32), slots], shares, chosen)

time: 51.8 us -> 52 us (level)
  waiting for transfers between devices: 1.36 us -> 0.62 us
  blocking collectives: 24.8 us -> 25.4 us
    all_to_all x1, waiting for transfers between devices: 1.36 us -> 0.62 us  [exchange(): return lax.all_to_all(x, axis, 0, 0, axis_index_groups=[group], tiled=True)]
    all_to_all x2, blocking collectives: 24.8 us -> 25.4 us  [exchange(): return lax.all_to_all(x, axis, 0, 0, axis_index_groups=[group], tiled=True)]
  transfers between devices with their start and end apart: 1 -> 1, of which waited for: 1 -> 1; matrix products, arithmetic and copies ran while one was open for 0% -> 0% of each run, Pallas kernels for 6% -> 8%
where the time goes in v6:
time: 52 us; the launch traced here: 51.7 us
  blocking collectives  25.4 us (49%)
  starting transfers between devices  16.7 us (32%)
  Pallas kernels  8.87 us (17%)
  waiting for transfers between devices  0.62 us (1%)
    all_to_all x2, blocking collectives, exchange(): return lax.all_to_all(x, axis, 0, 0, axis_index_groups=[group], tiled=True)  25.4 us
    all_to_all x1, starting transfers between devices, exchange(): return lax.all_to_all(x, axis, 0, 0, axis_index_groups=[group], tiled=True)  16.7 us
    pallas_call x5, Pallas kernels, call(): pl.pallas_call(kernel, out_shape=outs, in_specs=[NEAR] * len(args) + [ANY...  8.87 us
  transfers between devices with their start and end apart: 1, of which 1 were waited for; matrix products, arithmetic and copies ran while one was open for 0% of the time, Pallas kernels for 8%

profile of v6, /device:TPU:1, one launch (start us, length us, event | category | flops | bytes accessed | tf_op | source)
XLA Modules:
  0.0 51.7 jit_solution(1937407540947628687)
XLA Ops:
  0.0 1.7 %shard_map.65 = bf16[256,128]{1,0:T(8,128)(2,1)} custom-call(s32[8,128]{1,0:T(8,128)} %bitcast.11, s32[8,128]{1,0:T(8,128)} %bitcast.13, bf16[16,320]{1,0:T(8,128)(2,1)} %queries_hbm.3, bf16[16,160]{1,0:T(8,128)(2,1)} %fresh_hbm.3), custom_call_target="tpu_custom_call" | custom-call | tf_op jit(solution)/shard_map/pallas_call | solution.py:307
  1.7 16.7 %all-to-all-start = ((bf16[64,4,128]{2,1,0:T(4,128)(2,1)}), bf16[64,4,128]{2,1,0:T(4,128)(2,1)S(1)}, u32[]{:S(2)}, u32[]{:S(2)}) async-start(bf16[64,4,128]{2,1,0:T(4,128)(2,1)} %bitcast.3), calls=%async_computation | async-start | bytes 131072 | tf_op jit(solution)/shard_map/all_to_all | solution.py:294
  18.5 3.9 %shard_map.64 = (bf16[160,6400]{1,0:T(8,128)(2,1)S(1)}, bf16[256,2560]{1,0:T(8,128)(2,1)S(1)}, f32[8,320]{1,0:T(8,128)S(1)}, bf16[256,128]{1,0:T(8,128)(2,1)S(1)...) custom-call(s32[8,128]{1,0:T(8,128)} %bitcast.12, s32[8,128]{1,0:T(8,128)} %bitcast.14, ...), custom_call_target="tpu_custom_call" | custom-call | tf_op jit(solution)/shard_map/pallas_call | solution.py:307
  22.4 0.6 %all-to-all-done = bf16[64,4,128]{2,1,0:T(4,128)(2,1)S(1)} async-done(((bf16[64,4,128]{2,1,0:T(4,128)(2,1)}), bf16[64,4,128]{2,1,0:T(4,128)(2,1)S(1)}, u32[]{:S(2)}, u32[]{:S(2)}) %all-to-all-start) | async-done | bytes 65568 | tf_op jit(solution)/shard_map/all_to_all | solution.py:294
  23.0 2.3 %shard_map.66 = bf16[8,40,128]{2,1,0:T(8,128)(2,1)S(1)} custom-call(bf16[256,128]{1,0:T(8,128)(2,1)S(1)} %bitcast.7, bf16[32,256]{1,0:T(8,128)(2,1)S(1)} %get-tuple-element.15.chosen_t_ref, s32[8,128]{1,0:T(8,128)S(1)} %get-tuple-element.16.long_start_ref, f32[8,320]{1,0:T(8,128)S(1)} %get-tuple-element.17.home_ref, ...), custom_call_target="tpu_custom_call" | custom-call | tf_op jit(solution)/shard_map/pallas_call | solution.py:307
  25.3 10.6 %all_to_all.15.shares_ref = bf16[8,40,128]{2,1,0:T(8,128)(2,1)S(1)} all-to-all(bf16[8,40,128]{2,1,0:T(8,128)(2,1)S(1)} %shard_map.66), channel_id=1, replica_groups={{4,5,6,7,0,1,2,3},{12,13,14,15,8,9,10,11},{20,21,22,23,16,17,18,19},{28..., dimensions={0} | all-to-all | bytes 163840 | tf_op jit(solution)/shard_map/all_to_all | solution.py:294
  35.9 0.1 shard_map.67
  36.1 14.8 %all_to_all.16 = bf16[64,4,128]{2,1,0:T(4,128)(2,1)S(1)} all-to-all(bf16[64,4,128]{2,1,0:T(4,128)(2,1)S(1)} %bitcast.9), channel_id=1, replica_groups={{416,424,432,440,448,456,464,472,480,488,496,504,0,8,16,24,32,40,48,56,..., dimensions={0} | all-to-all | bytes 131072 | tf_op jit(solution)/shard_map/all_to_all | solution.py:294
  50.9 0.8 %shard_map.68 = bf16[16,320]{1,0:T(8,128)(2,1)} custom-call(bf16[32,256]{1,0:T(8,128)(2,1)S(1)} %get-tuple-element.14.placed_t_ref, f32[40,128]{1,0:T(8,128)S(1)} %get-tuple-element.21.home_ref, bf16[256,128]{1,0:T(8,128)(2,1)S(1)} %bitcast.8), custom_call_target="tpu_custom_call" | custom-call | tf_op jit(solution)/shard_map/pallas_call | solution.py:307
Async XLA Ops:
  1.7 21.3 %all-to-all-start = ((bf16[64,4,128]{2,1,0:T(4,128)(2,1)}), bf16[64,4,128]{2,1,0:T(4,128)(2,1)S(1)}, u32[]{:S(2)}, u32[]{:S(2)}) async-start(bf16[64,4,128]{2,1,0:T(4,128)(2,1)} %bitcast.3), calls=%async_computation | async-start | bytes 131072 | tf_op jit(solution)/shard_map/all_to_all | solution.py:294

commit v7 on v6

--- a/solution.py
+++ b/solution.py
@@ -177,14 +177,16 @@
         jnp.concatenate(own, axis=0),
         jnp.concatenate([fresh_value] * G, axis=0),
     )
+    count = starts.shape[0]
     return jnp.concatenate(
-        [jnp.where(is_long, long_out[g : g + 1], outs[g * 8 : g * 8 + 8]) for g in range(G)], axis=1
-    )
-
-
-def home_kernel(
+        [jnp.where(is_long, long_out[g : g + 1], outs[g * count : (g + 1) * count]) for g in range(G)],
+        axis=1,
+    )
+
+
+def load_kernel(
     offsets_hbm, lengths_hbm, queries_hbm, fresh_hbm, cache_hbm, weight_hbm,
-    near_ref, weight_ref, home_ref, chosen_ref, chosen_t_ref, placed_t_ref, long_start_ref,
+    near_ref, weight_ref, home_queries_ref, home_fresh_ref, numbers_ref, chosen_ref, chosen_t_ref, placed_t_ref,
     offsets_ref, lengths_ref, queries_ref, fresh_ref, sems, weight_sems, near_sems,
 ):
     sources = (offsets_hbm, lengths_hbm, queries_hbm, fresh_hbm)
@@ -206,7 +208,6 @@
     sources.append(cache_hbm.at[:, pl.ds(base, W + LANES)])
     targets.append(near_ref.at[:, pl.ds(len(blocks) * LANES, W + LANES)])
     near_copies = fetch(sources, targets, near_sems)
-    long_start_ref[...] = jnp.full((8, LANES), long_start, I32)
     flags = jnp.where(held & ((iota((8, LANES), 1) & 15) >= HALF), 1.0, 0.0).astype(BF)
     source = (iota((rows, 8), 0) >> 2) + REQ_FIRST
     line = jnp.where(source < slots, source, source - slots) >> 3
@@ -230,30 +231,36 @@
     row = iota((32, rows), 0)
     col = iota((32, rows), 1)
     placed_t_ref[...] = jnp.where(((col >> 2) == far) & ((col & 3) == (row >> 3)), 1.0, 0.0).astype(BF)
+    numbers_ref[0:8] = jnp.broadcast_to(starts[:8] - index * tokens, (8, LANES))
+    numbers_ref[8:16] = jnp.broadcast_to(lengths[:8], (8, LANES))
+    numbers_ref[16:24] = jnp.full((8, LANES), long_start, I32)
     for copy in copies[2:]:
         copy.wait()
-    queries = queries_ref[...].astype(F32)[:8]
-    fresh = fresh_ref[...].astype(F32)[:8]
+    home_queries_ref[...] = queries_ref[...].astype(F32)[:8]
+    home_fresh_ref[...] = fresh_ref[...].astype(F32)[:8]
     for copy in near_copies:
         copy.wait()
-    home_ref[...] = attend(
-        queries, fresh[:, :HD], fresh[:, HD:], starts[:8] - index * tokens, lengths[:8],
-        long_start, tokens, near_ref,
-    )
     weight_copy.wait()
 
 
-def far_kernel(
-    tokens, got_ref, chosen_t_ref, long_start_ref, home_ref, near_ref, weight_ref, weight_hbm, out_ref,
-    rest_ref, sems,
+def attend_kernel(
+    tokens, got_ref, chosen_t_ref, home_queries_ref, home_fresh_ref, numbers_ref, near_ref, weight_ref,
+    weight_hbm, out_ref, rest_ref, sems,
 ):
     upper, rest = weight_ref.shape[0], rest_ref.shape[0]
     (copy,) = fetch((weight_hbm.at[pl.ds(upper, rest)],), (rest_ref,), sems)
-    held = dot(chosen_t_ref[...], got_ref[...])
-    far = attend(*unpack(held), jnp.max(long_start_ref[0:1, :]), tokens, near_ref)
-    attended = jnp.concatenate([home_ref[...], far], axis=0).astype(BF)
+    numbers = numbers_ref[...]
+    long_start = jnp.max(numbers[16:17])
+    far = unpack(dot(chosen_t_ref[...], got_ref[...]))
+    home_fresh = home_fresh_ref[...]
+    home = (
+        home_queries_ref[...], home_fresh[:, :HD], home_fresh[:, HD:], numbers[:8, :1], numbers[8:16, :1]
+    )
+    both = [jnp.concatenate(pair, axis=0) for pair in zip(home, far)]
+    attended = attend(*both, long_start, tokens, near_ref).astype(BF)
+    mixed = dot(attended[:, :upper], weight_ref[...])
     copy.wait()
-    mixed = dot(attended[:, :upper], weight_ref[...]) + dot(attended[:, upper:], rest_ref[...])
+    mixed = mixed + dot(attended[:, upper:], rest_ref[...])
     columns = out_ref.shape[0]
     low = iota((HALF, LANES), 1) < 64
     for j in range(columns):
@@ -294,16 +301,16 @@
     return lax.all_to_all(x, axis, 0, 0, axis_index_groups=[group], tiled=True)
 
 
-def near(x):
+def in_vmem(x):
     return pltpu.with_memory_space_constraint(x, pltpu.VMEM)
 
 
-def held_back(x):
+def in_hbm(x):
     return pltpu.with_memory_space_constraint(x, pltpu.HBM)
 
 
-def call(kernel, out_shape, *args, far_args=(), scratch=(), in_hbm=False):
-    outs = out_shape if in_hbm else [pltpu.VMEM(s.shape, s.dtype) for s in out_shape]
+def call(kernel, out_shape, *args, far_args=(), scratch=(), result_in_hbm=False):
+    outs = out_shape if result_in_hbm else [pltpu.VMEM(s.shape, s.dtype) for s in out_shape]
     return pl.pallas_call(
         kernel,
         out_shape=outs,
@@ -311,7 +318,7 @@
         out_specs=[NEAR] * len(out_shape),
         scratch_shapes=scratch,
         compiler_params=pltpu.CompilerParams(vmem_limit_bytes=16 << 20),
-    )(*(near(a) for a in args), *(held_back(a) for a in far_args))
+    )(*(in_vmem(a) for a in args), *(in_hbm(a) for a in far_args))
 
 
 def shards(queries, fresh_kv, kv_cache, out_weight, offsets, lengths):
@@ -336,16 +343,17 @@
     got = exchange(message.reshape(devices, 4, LANES), "req", REQ_FIRST)
     near_blocks = (tokens - LMAX) // LANES + 1
     upper = out_weight.shape[0] * 4 // 5
-    home_near, home_weight, home_out, chosen, chosen_t, placed_t, long_start = call(
-        home_kernel,
+    near, weight, home_queries, home_fresh, numbers, chosen, chosen_t, placed_t = call(
+        load_kernel,
         [
             shape((2 * HD, near_blocks * LANES + W + LANES), BF),
             shape((upper, out_weight.shape[1]), BF),
             shape((HALF, width), F32),
+            shape((HALF, fresh_kv.shape[1]), F32),
+            shape((3 * HALF, LANES), I32),
             slots,
             shape((32, devices * 4), BF),
             shape((32, devices * 4), BF),
-            shape((8, LANES), I32),
         ],
         far_args=(*inputs, cache, out_weight),
         scratch=[
@@ -353,9 +361,9 @@
         ],
     )
     (shares,) = call(
-        functools.partial(far_kernel, tokens),
+        functools.partial(attend_kernel, tokens),
         [shape((columns, 40, LANES), BF)],
-        got.reshape(devices * 4, LANES), chosen_t, long_start, home_out, home_near, home_weight,
+        got.reshape(devices * 4, LANES), chosen_t, home_queries, home_fresh, numbers, near, weight,
         far_args=(out_weight,),
         scratch=[
             pltpu.VMEM((out_weight.shape[0] - upper, out_weight.shape[1]), BF), semaphores((1,))
@@ -368,7 +376,7 @@
         pick_kernel,
         [shape((row_count, width), BF)],
         placed_t, home, returned.reshape(devices * 4, LANES),
-        in_hbm=True,
+        result_in_hbm=True,
     )
     return mixed
 

time: 52 us -> 51.5 us (level)
  waiting for transfers between devices: 0.62 us -> 1.76 us
  Pallas kernels: 8.87 us -> 7.79 us
  blocking collectives: 25.4 us -> 24.8 us
    all_to_all x1, waiting for transfers between devices: 0.62 us -> 1.76 us  [exchange(): return lax.all_to_all(x, axis, 0, 0, axis_index_groups=[group], tiled=True)]
    pallas_call x5, Pallas kernels: 8.87 us -> 7.79 us  [call(): pl.pallas_call(kernel, out_shape=outs, in_specs=[NEAR] * len(args) + [ANY...]
    all_to_all x2, blocking collectives: 25.4 us -> 24.8 us  [exchange(): return lax.all_to_all(x, axis, 0, 0, axis_index_groups=[group], tiled=True)]
  transfers between devices with their start and end apart: 1 -> 1, of which waited for: 1 -> 1; matrix products, arithmetic and copies ran while one was open for 0% -> 0% of each run, Pallas kernels for 8% -> 5%
where the time goes in v7:
time: 51.5 us; the launch traced here: 51.1 us
  blocking collectives  24.8 us (48%)
  starting transfers between devices  16.7 us (32%)
  Pallas kernels  7.79 us (15%)
  waiting for transfers between devices  1.76 us (3%)
    all_to_all x2, blocking collectives, exchange(): return lax.all_to_all(x, axis, 0, 0, axis_index_groups=[group], tiled=True)  24.8 us
    all_to_all x1, starting transfers between devices, exchange(): return lax.all_to_all(x, axis, 0, 0, axis_index_groups=[group], tiled=True)  16.7 us
    pallas_call x5, Pallas kernels, call(): pl.pallas_call(kernel, out_shape=outs, in_specs=[NEAR] * len(args) + [ANY...  7.79 us
    all_to_all x1, waiting for transfers between devices, exchange(): return lax.all_to_all(x, axis, 0, 0, axis_index_groups=[group], tiled=True)  1.76 us
  transfers between devices with their start and end apart: 1, of which 1 were waited for; matrix products, arithmetic and copies ran while one was open for 0% of the time, Pallas kernels for 5%

profile of v7, /device:TPU:1, one launch (start us, length us, event | category | flops | bytes accessed | tf_op | source)
XLA Modules:
  0.0 51.1 jit_solution(3791011640797912433)
XLA Ops:
  0.0 1.7 %shard_map.65 = bf16[256,128]{1,0:T(8,128)(2,1)} custom-call(s32[8,128]{1,0:T(8,128)} %bitcast.11, s32[8,128]{1,0:T(8,128)} %bitcast.13, bf16[16,320]{1,0:T(8,128)(2,1)} %queries_hbm.3, bf16[16,160]{1,0:T(8,128)(2,1)} %fresh_hbm.3), custom_call_target="tpu_custom_call" | custom-call | tf_op jit(solution)/shard_map/pallas_call | solution.py:314
  1.7 16.7 %all-to-all-start = ((bf16[64,4,128]{2,1,0:T(4,128)(2,1)}), bf16[64,4,128]{2,1,0:T(4,128)(2,1)S(1)}, u32[]{:S(2)}, u32[]{:S(2)}) async-start(bf16[64,4,128]{2,1,0:T(4,128)(2,1)} %bitcast.3), calls=%async_computation | async-start | bytes 131072 | tf_op jit(solution)/shard_map/all_to_all | solution.py:301
  18.5 2.8 %shard_map.64 = (bf16[160,6400]{1,0:T(8,128)(2,1)S(1)}, bf16[256,2560]{1,0:T(8,128)(2,1)S(1)}, f32[8,320]{1,0:T(8,128)S(1)}, f32[8,160]{1,0:T(8,128)S(1)}, s32[2...) custom-call(s32[8,128]{1,0:T(8,128)} %bitcast.12, ...), custom_call_target="tpu_custom_call" | custom-call | tf_op jit(solution)/shard_map/pallas_call | solution.py:314
  21.3 1.8 %all-to-all-done = bf16[64,4,128]{2,1,0:T(4,128)(2,1)S(1)} async-done(((bf16[64,4,128]{2,1,0:T(4,128)(2,1)}), bf16[64,4,128]{2,1,0:T(4,128)(2,1)S(1)}, u32[]{:S(2)}, u32[]{:S(2)}) %all-to-all-start) | async-done | bytes 65568 | tf_op jit(solution)/shard_map/all_to_all | solution.py:301
  23.0 2.3 %shard_map.66 = bf16[8,40,128]{2,1,0:T(8,128)(2,1)S(1)} custom-call(bf16[256,128]{1,0:T(8,128)(2,1)S(1)} %bitcast.7, bf16[32,256]{1,0:T(8,128)(2,1)S(1)} %get-tuple-element.16.chosen_t_ref, f32[8,320]{1,0:T(8,128)S(1)} %get-tuple-element.17.home_queries_ref, f32[8,160]{1,0:T(8,128)S(1)} %get-tuple-element.18.home_fresh_ref, ...), custom_call_target="tpu_custom_call" | custom-call | tf_op jit(solution)/shard_map/pallas_call | solution.py:314
  25.3 10.6 %all_to_all.15.shares_ref = bf16[8,40,128]{2,1,0:T(8,128)(2,1)S(1)} all-to-all(bf16[8,40,128]{2,1,0:T(8,128)(2,1)S(1)} %shard_map.66), channel_id=1, replica_groups={{4,5,6,7,0,1,2,3},{12,13,14,15,8,9,10,11},{20,21,22,23,16,17,18,19},{28..., dimensions={0} | all-to-all | bytes 163840 | tf_op jit(solution)/shard_map/all_to_all | solution.py:301
  36.0 0.1 shard_map.67
  36.1 14.2 %all_to_all.16 = bf16[64,4,128]{2,1,0:T(4,128)(2,1)S(1)} all-to-all(bf16[64,4,128]{2,1,0:T(4,128)(2,1)S(1)} %bitcast.9), channel_id=1, replica_groups={{416,424,432,440,448,456,464,472,480,488,496,504,0,8,16,24,32,40,48,56,..., dimensions={0} | all-to-all | bytes 131072 | tf_op jit(solution)/shard_map/all_to_all | solution.py:301
  50.3 0.8 %shard_map.68 = bf16[16,320]{1,0:T(8,128)(2,1)} custom-call(bf16[32,256]{1,0:T(8,128)(2,1)S(1)} %get-tuple-element.15.placed_t_ref, f32[40,128]{1,0:T(8,128)S(1)} %get-tuple-element.23.home_ref, bf16[256,128]{1,0:T(8,128)(2,1)S(1)} %bitcast.8), custom_call_target="tpu_custom_call" | custom-call | tf_op jit(solution)/shard_map/pallas_call | solution.py:314
Async XLA Ops:
  1.7 21.3 %all-to-all-start = ((bf16[64,4,128]{2,1,0:T(4,128)(2,1)}), bf16[64,4,128]{2,1,0:T(4,128)(2,1)S(1)}, u32[]{:S(2)}, u32[]{:S(2)}) async-start(bf16[64,4,128]{2,1,0:T(4,128)(2,1)} %bitcast.3), calls=%async_computation | async-start | bytes 131072 | tf_op jit(solution)/shard_map/all_to_all | solution.py:301

commit v8 on v7

--- a/solution.py
+++ b/solution.py
@@ -2,6 +2,7 @@
 
 import jax
 import jax.numpy as jnp
+import numpy as np
 from jax import lax
 from jax.experimental import pallas as pl
 from jax.experimental.pallas import tpu as pltpu
@@ -13,7 +14,7 @@
 LMAX = 8192
 LANES = 128
 HALF = 8
-REQ_FIRST = 52
+FIRST_Z, FIRST_X, FIRST_CORE = 6, 2, 1
 TP_FIRST = 4
 BF = jnp.bfloat16
 F32 = jnp.float32
@@ -82,8 +83,21 @@
     return copies
 
 
-def slot_of(owners, slots):
-    return jnp.where(owners < REQ_FIRST, owners + (slots - REQ_FIRST), owners - REQ_FIRST)
+def source_of(slot, where=jnp.where):
+    place = (slot + 63) & 63
+    ring_z, ring_x = place >> 3, (place >> 1) & 3
+    z = FIRST_Z + 4 + where((ring_z & 1) == 1, -((ring_z + 1) >> 1), ring_z >> 1)
+    x = FIRST_X + 2 + where((ring_x & 1) == 1, -((ring_x + 1) >> 1), ring_x >> 1)
+    return (z & 7) * 8 + (x & 3) * 2 + ((FIRST_CORE + 1 + place) & 1)
+
+
+def slot_of(member):
+    z = (((member >> 3) - FIRST_Z) & 7) - 4
+    x = ((((member >> 1) & 3) - FIRST_X) & 3) - 2
+    ring_z = jnp.where(z < 0, -2 * z - 1, 2 * z)
+    ring_x = jnp.where(x < 0, -2 * x - 1, 2 * x)
+    core = (member + FIRST_CORE + 1) & 1
+    return (ring_z * 8 + ring_x * 2 + core + 1) & 63
 
 
 def send_kernel(
@@ -99,7 +113,7 @@
     owners = owner_of(offsets, tokens)
     starts = column(offsets - owners * tokens, HALF)
     lengths = column(own_row(lengths_ref, index, HALF), HALF)
-    far = slot_of(owners, rows // 4)
+    far = slot_of(owners)
     lane = iota((1, LANES), 1)
     spread = jnp.where(lane < 8, far, 0)
     for k in (1, 2, 3):
@@ -198,7 +212,6 @@
     index = lax.axis_index("req")
     tokens = cache_hbm.shape[1]
     rows = chosen_ref.shape[0]
-    slots = rows // 4
     offsets = offsets_ref[...]
     held = owner_of(offsets, tokens) == index
     long_start = jnp.sum(jnp.where(held & (lengths_ref[...] == LMAX), offsets, 0)) - index * tokens
@@ -209,14 +222,12 @@
     targets.append(near_ref.at[:, pl.ds(len(blocks) * LANES, W + LANES)])
     near_copies = fetch(sources, targets, near_sems)
     flags = jnp.where(held & ((iota((8, LANES), 1) & 15) >= HALF), 1.0, 0.0).astype(BF)
-    source = (iota((rows, 8), 0) >> 2) + REQ_FIRST
-    line = jnp.where(source < slots, source, source - slots) >> 3
+    line = source_of(iota((rows, 8), 0) >> 2) >> 3
     here = dot(jnp.where(line == iota((rows, 8), 1), 1.0, 0.0).astype(BF), flags)
     earlier = dot(jnp.where(line > iota((rows, 8), 1), 1.0, 0.0).astype(BF), flags)
     row = iota((rows, LANES), 0)
     col = iota((rows, LANES), 1)
-    source = (row >> 2) + REQ_FIRST
-    slot = jnp.where(source < slots, source, source - slots) & 7
+    slot = source_of(row >> 2) & 7
     valid = jnp.sum(jnp.where((col >> 4) == slot, here, 0.0), axis=1, keepdims=True)
     rank = jnp.sum(earlier + jnp.where((col >> 4) < slot, here, 0.0), axis=1, keepdims=True)
     hit = (valid > 0.5) & (rank.astype(I32) == (col & 7)) & ((row & 3) == (col >> 3))
@@ -226,7 +237,7 @@
     offsets = own_row(offsets_ref, index, 0)
     starts = column(offsets, 16)
     lengths = column(own_row(lengths_ref, index, 0), 16)
-    far = slot_of(owner_of(starts[8:], tokens), slots)
+    far = slot_of(owner_of(starts[8:], tokens))
     far = jnp.concatenate([far] * 4, axis=0)
     row = iota((32, rows), 0)
     col = iota((32, rows), 1)
@@ -295,9 +306,7 @@
     out_ref[...] = jnp.where(odd, jnp.concatenate([half, first, second], axis=1), even).astype(BF)
 
 
-def exchange(x, axis, first):
-    size = lax.axis_size(axis)
-    group = [(first + i) % size for i in range(size)]
+def exchange(x, axis, group):
     return lax.all_to_all(x, axis, 0, 0, axis_index_groups=[group], tiled=True)
 
 
@@ -324,6 +333,7 @@
 def shards(queries, fresh_kv, kv_cache, out_weight, offsets, lengths):
     devices = lax.axis_size("req")
     columns = lax.axis_size("tp")
+    req_group = [int(i) for i in source_of(np.arange(devices), np.where)]
     row_count, width = queries.shape
     tokens = kv_cache.shape[2]
     cache = kv_cache.reshape(kv_cache.shape[1:])
@@ -340,7 +350,7 @@
         far_args=inputs,
         scratch=[*map(scratch, inputs), semaphores((4,))],
     )
-    got = exchange(message.reshape(devices, 4, LANES), "req", REQ_FIRST)
+    got = exchange(message.reshape(devices, 4, LANES), "req", req_group)
     near_blocks = (tokens - LMAX) // LANES + 1
     upper = out_weight.shape[0] * 4 // 5
     near, weight, home_queries, home_fresh, numbers, chosen, chosen_t, placed_t = call(
@@ -369,9 +379,9 @@
             pltpu.VMEM((out_weight.shape[0] - upper, out_weight.shape[1]), BF), semaphores((1,))
         ],
     )
-    shares = exchange(shares, "tp", TP_FIRST)
+    shares = exchange(shares, "tp", [(TP_FIRST + i) % columns for i in range(columns)])
     home, spread = call(spread_kernel, [shape((40, LANES), F32), slots], shares, chosen)
-    returned = exchange(spread.reshape(devices, 4, LANES), "req", REQ_FIRST)
+    returned = exchange(spread.reshape(devices, 4, LANES), "req", req_group)
     (mixed,) = call(
         pick_kernel,
         [shape((row_count, width), BF)],

time: 51.5 us -> 50.6 us (0.983)
  transfers between devices with their start and end apart: 1 -> 1, of which waited for: 1 -> 1; matrix products, arithmetic and copies ran while one was open for 0% -> 0% of each run, Pallas kernels for 5% -> 6%
where the time goes in v8:
time: 50.6 us; the launch traced here: 50.3 us
  blocking collectives  24.5 us (48%)
  starting transfers between devices  16.4 us (32%)
  Pallas kernels  7.89 us (16%)
  waiting for transfers between devices  1.54 us (3%)
    all_to_all x2, blocking collectives, exchange(): return lax.all_to_all(x, axis, 0, 0, axis_index_groups=[group], tiled=True)  24.5 us
    all_to_all x1, starting transfers between devices, exchange(): return lax.all_to_all(x, axis, 0, 0, axis_index_groups=[group], tiled=True)  16.4 us
    pallas_call x5, Pallas kernels, call(): pl.pallas_call(kernel, out_shape=outs, in_specs=[NEAR] * len(args) + [ANY...  7.89 us
    all_to_all x1, waiting for transfers between devices, exchange(): return lax.all_to_all(x, axis, 0, 0, axis_index_groups=[group], tiled=True)  1.54 us
  transfers between devices with their start and end apart: 1, of which 1 were waited for; matrix products, arithmetic and copies ran while one was open for 0% of the time, Pallas kernels for 6%

profile of v8, /device:TPU:1, one launch (start us, length us, event | category | flops | bytes accessed | tf_op | source)
XLA Modules:
  0.0 50.3 jit_solution(17612478448061252618)
XLA Ops:
  0.0 1.7 %shard_map.65 = bf16[256,128]{1,0:T(8,128)(2,1)} custom-call(s32[8,128]{1,0:T(8,128)} %bitcast.11, s32[8,128]{1,0:T(8,128)} %bitcast.13, bf16[16,320]{1,0:T(8,128)(2,1)} %queries_hbm.3, bf16[16,160]{1,0:T(8,128)(2,1)} %fresh_hbm.3), custom_call_target="tpu_custom_call" | custom-call | tf_op jit(solution)/shard_map/pallas_call | solution.py:323
  1.7 16.4 %all-to-all-start = ((bf16[64,4,128]{2,1,0:T(4,128)(2,1)}), bf16[64,4,128]{2,1,0:T(4,128)(2,1)S(1)}, u32[]{:S(2)}, u32[]{:S(2)}) async-start(bf16[64,4,128]{2,1,0:T(4,128)(2,1)} %bitcast.3), calls=%async_computation | async-start | bytes 131072 | tf_op jit(solution)/shard_map/all_to_all | solution.py:310
  18.1 2.9 %shard_map.64 = (bf16[160,6400]{1,0:T(8,128)(2,1)S(1)}, bf16[256,2560]{1,0:T(8,128)(2,1)S(1)}, f32[8,320]{1,0:T(8,128)S(1)}, f32[8,160]{1,0:T(8,128)S(1)}, s32[2...) custom-call(s32[8,128]{1,0:T(8,128)} %bitcast.12, ...), custom_call_target="tpu_custom_call" | custom-call | tf_op jit(solution)/shard_map/pallas_call | solution.py:323
  21.0 1.5 %all-to-all-done = bf16[64,4,128]{2,1,0:T(4,128)(2,1)S(1)} async-done(((bf16[64,4,128]{2,1,0:T(4,128)(2,1)}), bf16[64,4,128]{2,1,0:T(4,128)(2,1)S(1)}, u32[]{:S(2)}, u32[]{:S(2)}) %all-to-all-start) | async-done | bytes 65568 | tf_op jit(solution)/shard_map/all_to_all | solution.py:310
  22.5 2.3 %shard_map.66 = bf16[8,40,128]{2,1,0:T(8,128)(2,1)S(1)} custom-call(bf16[256,128]{1,0:T(8,128)(2,1)S(1)} %bitcast.7, bf16[32,256]{1,0:T(8,128)(2,1)S(1)} %get-tuple-element.16.chosen_t_ref, f32[8,320]{1,0:T(8,128)S(1)} %get-tuple-element.17.home_queries_ref, f32[8,160]{1,0:T(8,128)S(1)} %get-tuple-element.18.home_fresh_ref, ...), custom_call_target="tpu_custom_call" | custom-call | tf_op jit(solution)/shard_map/pallas_call | solution.py:323
  24.9 10.6 %all_to_all.15.shares_ref = bf16[8,40,128]{2,1,0:T(8,128)(2,1)S(1)} all-to-all(bf16[8,40,128]{2,1,0:T(8,128)(2,1)S(1)} %shard_map.66), channel_id=1, replica_groups={{4,5,6,7,0,1,2,3},{12,13,14,15,8,9,10,11},{20,21,22,23,16,17,18,19},{28..., dimensions={0} | all-to-all | bytes 163840 | tf_op jit(solution)/shard_map/all_to_all | solution.py:310
  35.5 0.1 shard_map.67
  35.7 13.8 %all_to_all.16 = bf16[64,4,128]{2,1,0:T(4,128)(2,1)S(1)} all-to-all(bf16[64,4,128]{2,1,0:T(4,128)(2,1)S(1)} %bitcast.9), channel_id=1, replica_groups={{424,128,136,176,184,144,152,160,168,64,72,112,120,80,88,96,104,192,200..., dimensions={0} | all-to-all | bytes 131072 | tf_op jit(solution)/shard_map/all_to_all | solution.py:310
  49.5 0.8 %shard_map.68 = bf16[16,320]{1,0:T(8,128)(2,1)} custom-call(bf16[32,256]{1,0:T(8,128)(2,1)S(1)} %get-tuple-element.15.placed_t_ref, f32[40,128]{1,0:T(8,128)S(1)} %get-tuple-element.23.home_ref, bf16[256,128]{1,0:T(8,128)(2,1)S(1)} %bitcast.8), custom_call_target="tpu_custom_call" | custom-call | tf_op jit(solution)/shard_map/pallas_call | solution.py:323
Async XLA Ops:
  1.7 20.8 %all-to-all-start = ((bf16[64,4,128]{2,1,0:T(4,128)(2,1)}), bf16[64,4,128]{2,1,0:T(4,128)(2,1)S(1)}, u32[]{:S(2)}, u32[]{:S(2)}) async-start(bf16[64,4,128]{2,1,0:T(4,128)(2,1)} %bitcast.3), calls=%async_computation | async-start | bytes 131072 | tf_op jit(solution)/shard_map/all_to_all | solution.py:310

commit v9 on v8

--- a/solution.py
+++ b/solution.py
@@ -112,7 +112,6 @@
     offsets = own_row(offsets_ref, index, HALF)
     owners = owner_of(offsets, tokens)
     starts = column(offsets - owners * tokens, HALF)
-    lengths = column(own_row(lengths_ref, index, HALF), HALF)
     far = slot_of(owners)
     lane = iota((1, LANES), 1)
     spread = jnp.where(lane < 8, far, 0)
@@ -123,6 +122,7 @@
     col = iota((rows, LANES), 1)
     hit = ((row >> 2) == jnp.broadcast_to(spread, (rows, LANES))) & ((row & 3) == (col >> 3))
     placed = jnp.where(hit, 1.0, 0.0).astype(BF)
+    lengths = column(own_row(lengths_ref, index, HALF), HALF)
     queries = queries_ref[...].astype(F32)
     fresh = fresh_ref[...].astype(F32)
     stack = pack(queries[8:], fresh[8:], starts, lengths)
@@ -153,11 +153,14 @@
     return blocks, first, pl.multiple_of(base, LANES)
 
 
-def attend(queries, fresh_key, fresh_value, starts, lengths, long_start, tokens, near_ref):
+def split(queries, fresh_key):
+    heads = [queries[:, g * HD : (g + 1) * HD] for g in range(G)]
+    return heads, [jnp.sum(h * fresh_key, axis=1, keepdims=True) * HD ** (-0.5) for h in heads]
+
+
+def attend(heads, own, fresh_value, starts, lengths, long_start, tokens, near_ref):
     blocks, first, base = places(long_start, tokens)
     others, span = len(blocks) * LANES, W + LANES
-    heads = [queries[:, g * HD : (g + 1) * HD] for g in range(G)]
-    own = [jnp.sum(h * fresh_key, axis=1, keepdims=True) * HD ** (-0.5) for h in heads]
     is_long = lengths == LMAX
     long_query = jnp.zeros((8, HD), F32)
     long_own = jnp.zeros((8, 1), F32)
@@ -200,7 +203,7 @@
 
 def load_kernel(
     offsets_hbm, lengths_hbm, queries_hbm, fresh_hbm, cache_hbm, weight_hbm,
-    near_ref, weight_ref, home_queries_ref, home_fresh_ref, numbers_ref, chosen_ref, chosen_t_ref, placed_t_ref,
+    near_ref, weight_ref, home_ref, chosen_ref, chosen_t_ref, placed_t_ref,
     offsets_ref, lengths_ref, queries_ref, fresh_ref, sems, weight_sems, near_sems,
 ):
     sources = (offsets_hbm, lengths_hbm, queries_hbm, fresh_hbm)
@@ -242,33 +245,45 @@
     row = iota((32, rows), 0)
     col = iota((32, rows), 1)
     placed_t_ref[...] = jnp.where(((col >> 2) == far) & ((col & 3) == (row >> 3)), 1.0, 0.0).astype(BF)
-    numbers_ref[0:8] = jnp.broadcast_to(starts[:8] - index * tokens, (8, LANES))
-    numbers_ref[8:16] = jnp.broadcast_to(lengths[:8], (8, LANES))
-    numbers_ref[16:24] = jnp.full((8, LANES), long_start, I32)
     for copy in copies[2:]:
         copy.wait()
-    home_queries_ref[...] = queries_ref[...].astype(F32)[:8]
-    home_fresh_ref[...] = fresh_ref[...].astype(F32)[:8]
+    fresh = fresh_ref[...].astype(F32)[:8]
+    heads, own = split(queries_ref[...].astype(F32)[:8], fresh[:, :HD])
+    lane = iota((HALF, LANES), 1)
+    wide = lambda x: jnp.concatenate([x, jnp.zeros((HALF, LANES - HD), F32)], axis=1)
+    for g in range(G):
+        home_ref[g * HALF : (g + 1) * HALF] = jnp.where(lane == HD, own[g], wide(heads[g]))
+    last = wide(fresh[:, HD:])
+    numbers = (starts[:8] - index * tokens, lengths[:8], jnp.full((8, 1), long_start, I32))
+    for i, number in enumerate(numbers):
+        last = jnp.where(lane == HD + i, number.astype(F32), last)
+    home_ref[G * HALF :] = last
     for copy in near_copies:
         copy.wait()
     weight_copy.wait()
 
 
 def attend_kernel(
-    tokens, got_ref, chosen_t_ref, home_queries_ref, home_fresh_ref, numbers_ref, near_ref, weight_ref,
+    tokens, got_ref, chosen_t_ref, home_ref, near_ref, weight_ref,
     weight_hbm, out_ref, rest_ref, sems,
 ):
     upper, rest = weight_ref.shape[0], rest_ref.shape[0]
     (copy,) = fetch((weight_hbm.at[pl.ds(upper, rest)],), (rest_ref,), sems)
-    numbers = numbers_ref[...]
-    long_start = jnp.max(numbers[16:17])
-    far = unpack(dot(chosen_t_ref[...], got_ref[...]))
-    home_fresh = home_fresh_ref[...]
-    home = (
-        home_queries_ref[...], home_fresh[:, :HD], home_fresh[:, HD:], numbers[:8, :1], numbers[8:16, :1]
-    )
-    both = [jnp.concatenate(pair, axis=0) for pair in zip(home, far)]
-    attended = attend(*both, long_start, tokens, near_ref).astype(BF)
+    last = home_ref[G * HALF :]
+    numbers = last[:, HD : HD + 3].astype(I32)
+    long_start = jnp.max(numbers[:, 2:3])
+    queries, fresh_key, fresh_value, starts, lengths = unpack(dot(chosen_t_ref[...], got_ref[...]))
+    far_heads, far_own = split(queries, fresh_key)
+    stack = lambda *pair: jnp.concatenate(pair, axis=0)
+    rows = [slice(g * HALF, (g + 1) * HALF) for g in range(G)]
+    attended = attend(
+        [stack(home_ref[r, :HD], far) for r, far in zip(rows, far_heads)],
+        [stack(home_ref[r, HD : HD + 1], far) for r, far in zip(rows, far_own)],
+        stack(last[:, :HD], fresh_value),
+        stack(numbers[:, 0:1], starts),
+        stack(numbers[:, 1:2], lengths),
+        long_start, tokens, near_ref,
+    ).astype(BF)
     mixed = dot(attended[:, :upper], weight_ref[...])
     copy.wait()
     mixed = mixed + dot(attended[:, upper:], rest_ref[...])
@@ -353,14 +368,12 @@
     got = exchange(message.reshape(devices, 4, LANES), "req", req_group)
     near_blocks = (tokens - LMAX) // LANES + 1
     upper = out_weight.shape[0] * 4 // 5
-    near, weight, home_queries, home_fresh, numbers, chosen, chosen_t, placed_t = call(
+    near, weight, home, chosen, chosen_t, placed_t = call(
         load_kernel,
         [
             shape((2 * HD, near_blocks * LANES + W + LANES), BF),
             shape((upper, out_weight.shape[1]), BF),
-            shape((HALF, width), F32),
-            shape((HALF, fresh_kv.shape[1]), F32),
-            shape((3 * HALF, LANES), I32),
+            shape(((G + 1) * HALF, LANES), F32),
             slots,
             shape((32, devices * 4), BF),
             shape((32, devices * 4), BF),
@@ -373,7 +386,7 @@
     (shares,) = call(
         functools.partial(attend_kernel, tokens),
         [shape((columns, 40, LANES), BF)],
-        got.reshape(devices * 4, LANES), chosen_t, home_queries, home_fresh, numbers, near, weight,
+        got.reshape(devices * 4, LANES), chosen_t, home, near, weight,
         far_args=(out_weight,),
         scratch=[
             pltpu.VMEM((out_weight.shape[0] - upper, out_weight.shape[1]), BF), semaphores((1,))

time: 50.6 us -> 50.4 us (level)
  no operation moved by 1% of the time
where the time goes in v9:
time: 50.4 us; the launch traced here: 50.1 us
  blocking collectives  24.5 us (49%)
  starting transfers between devices  16.4 us (33%)
  Pallas kernels  7.71 us (15%)
  waiting for transfers between devices  1.54 us (3%)
    all_to_all x2, blocking collectives, exchange(): return lax.all_to_all(x, axis, 0, 0, axis_index_groups=[group], tiled=True)  24.5 us
    all_to_all x1, starting transfers between devices, exchange(): return lax.all_to_all(x, axis, 0, 0, axis_index_groups=[group], tiled=True)  16.4 us
    pallas_call x5, Pallas kernels, call(): pl.pallas_call(kernel, out_shape=outs, in_specs=[NEAR] * len(args) + [ANY...  7.71 us
    all_to_all x1, waiting for transfers between devices, exchange(): return lax.all_to_all(x, axis, 0, 0, axis_index_groups=[group], tiled=True)  1.54 us
  transfers between devices with their start and end apart: 1, of which 1 were waited for; matrix products, arithmetic and copies ran while one was open for 0% of the time, Pallas kernels for 6%

profile of v9, /device:TPU:1, one launch (start us, length us, event | category | flops | bytes accessed | tf_op | source)
XLA Modules:
  0.0 50.1 jit_solution(4181097017140348960)
XLA Ops:
  0.0 1.7 %shard_map.65 = bf16[256,128]{1,0:T(8,128)(2,1)} custom-call(s32[8,128]{1,0:T(8,128)} %bitcast.11, s32[8,128]{1,0:T(8,128)} %bitcast.13, bf16[16,320]{1,0:T(8,128)(2,1)} %queries_hbm.3, bf16[16,160]{1,0:T(8,128)(2,1)} %fresh_hbm.3), custom_call_target="tpu_custom_call" | custom-call | tf_op jit(solution)/shard_map/pallas_call | solution.py:338
  1.7 16.4 %all-to-all-start = ((bf16[64,4,128]{2,1,0:T(4,128)(2,1)}), bf16[64,4,128]{2,1,0:T(4,128)(2,1)S(1)}, u32[]{:S(2)}, u32[]{:S(2)}) async-start(bf16[64,4,128]{2,1,0:T(4,128)(2,1)} %bitcast.3), calls=%async_computation | async-start | bytes 131072 | tf_op jit(solution)/shard_map/all_to_all | solution.py:325
  18.1 2.9 %shard_map.64 = (bf16[160,6400]{1,0:T(8,128)(2,1)S(1)}, bf16[256,2560]{1,0:T(8,128)(2,1)S(1)}, f32[40,128]{1,0:T(8,128)S(1)}, bf16[256,128]{1,0:T(8,128)(2,1)S(1...) custom-call(s32[8,128]{1,0:T(8,128)} %bitcast.12, s32[8,128]{1,0:T(8,128)} %bitcast.14, ...), custom_call_target="tpu_custom_call" | custom-call | tf_op jit(solution)/shard_map/pallas_call | solution.py:338
  21.0 1.5 %all-to-all-done = bf16[64,4,128]{2,1,0:T(4,128)(2,1)S(1)} async-done(((bf16[64,4,128]{2,1,0:T(4,128)(2,1)}), bf16[64,4,128]{2,1,0:T(4,128)(2,1)S(1)}, u32[]{:S(2)}, u32[]{:S(2)}) %all-to-all-start) | async-done | bytes 65568 | tf_op jit(solution)/shard_map/all_to_all | solution.py:325
  22.5 2.1 %shard_map.66 = bf16[8,40,128]{2,1,0:T(8,128)(2,1)S(1)} custom-call(bf16[256,128]{1,0:T(8,128)(2,1)S(1)} %bitcast.7, bf16[32,256]{1,0:T(8,128)(2,1)S(1)} %get-tuple-element.14.chosen_t_ref, f32[40,128]{1,0:T(8,128)S(1)} %get-tuple-element.15.home_ref, bf16[160,6400]{1,0:T(8,128)(2,1)S(1)} %get-tuple-element.16.near_ref, ...), custom_call_target="tpu_custom_call" | custom-call | tf_op jit(solution)/shard_map/pallas_call | solution.py:338
  24.7 10.6 %all_to_all.15.shares_ref = bf16[8,40,128]{2,1,0:T(8,128)(2,1)S(1)} all-to-all(bf16[8,40,128]{2,1,0:T(8,128)(2,1)S(1)} %shard_map.66), channel_id=1, replica_groups={{4,5,6,7,0,1,2,3},{12,13,14,15,8,9,10,11},{20,21,22,23,16,17,18,19},{28..., dimensions={0} | all-to-all | bytes 163840 | tf_op jit(solution)/shard_map/all_to_all | solution.py:325
  35.3 0.1 shard_map.67
  35.5 13.8 %all_to_all.16 = bf16[64,4,128]{2,1,0:T(4,128)(2,1)S(1)} all-to-all(bf16[64,4,128]{2,1,0:T(4,128)(2,1)S(1)} %bitcast.9), channel_id=1, replica_groups={{424,128,136,176,184,144,152,160,168,64,72,112,120,80,88,96,104,192,200..., dimensions={0} | all-to-all | bytes 131072 | tf_op jit(solution)/shard_map/all_to_all | solution.py:325
  49.3 0.8 %shard_map.68 = bf16[16,320]{1,0:T(8,128)(2,1)} custom-call(bf16[32,256]{1,0:T(8,128)(2,1)S(1)} %get-tuple-element.13.placed_t_ref, f32[40,128]{1,0:T(8,128)S(1)} %get-tuple-element.19.home_ref, bf16[256,128]{1,0:T(8,128)(2,1)S(1)} %bitcast.8), custom_call_target="tpu_custom_call" | custom-call | tf_op jit(solution)/shard_map/pallas_call | solution.py:338
Async XLA Ops:
  1.7 20.8 %all-to-all-start = ((bf16[64,4,128]{2,1,0:T(4,128)(2,1)}), bf16[64,4,128]{2,1,0:T(4,128)(2,1)S(1)}, u32[]{:S(2)}, u32[]{:S(2)}) async-start(bf16[64,4,128]{2,1,0:T(4,128)(2,1)} %bitcast.3), calls=%async_computation | async-start | bytes 131072 | tf_op jit(solution)/shard_map/all_to_all | solution.py:325

commit v10 on v9

--- a/solution.py
+++ b/solution.py
@@ -15,7 +15,7 @@
 LANES = 128
 HALF = 8
 FIRST_Z, FIRST_X, FIRST_CORE = 6, 2, 1
-TP_FIRST = 4
+TP_GROUP = (5, 1, 2, 0, 3, 7, 4, 6)
 BF = jnp.bfloat16
 F32 = jnp.float32
 I32 = jnp.int32
@@ -298,7 +298,7 @@
         else:
             half = jnp.where(low, pltpu.roll(tiles[0][:8], 64, 1), tiles[0][8:])
             full = tiles[1:]
-        out_ref[(j - TP_FIRST) % columns] = jnp.concatenate([*full, half], axis=0).astype(BF)
+        out_ref[TP_GROUP.index(j)] = jnp.concatenate([*full, half], axis=0).astype(BF)
 
 
 def spread_kernel(shares_ref, chosen_ref, home_ref, out_ref):
@@ -392,7 +392,7 @@
             pltpu.VMEM((out_weight.shape[0] - upper, out_weight.shape[1]), BF), semaphores((1,))
         ],
     )
-    shares = exchange(shares, "tp", [(TP_FIRST + i) % columns for i in range(columns)])
+    shares = exchange(shares, "tp", list(TP_GROUP))
     home, spread = call(spread_kernel, [shape((40, LANES), F32), slots], shares, chosen)
     returned = exchange(spread.reshape(devices, 4, LANES), "req", req_group)
     (mixed,) = call(

time: 50.4 us -> 50.5 us (level)
  no operation moved by 1% of the time
where the time goes in v10:
time: 50.5 us; the launch traced here: 50.2 us
  blocking collectives  24.6 us (49%)
  starting transfers between devices  16.4 us (32%)
  Pallas kernels  7.71 us (15%)
  waiting for transfers between devices  1.54 us (3%)
    all_to_all x2, blocking collectives, exchange(): return lax.all_to_all(x, axis, 0, 0, axis_index_groups=[group], tiled=True)  24.6 us
    all_to_all x1, starting transfers between devices, exchange(): return lax.all_to_all(x, axis, 0, 0, axis_index_groups=[group], tiled=True)  16.4 us
    pallas_call x5, Pallas kernels, call(): pl.pallas_call(kernel, out_shape=outs, in_specs=[NEAR] * len(args) + [ANY...  7.71 us
    all_to_all x1, waiting for transfers between devices, exchange(): return lax.all_to_all(x, axis, 0, 0, axis_index_groups=[group], tiled=True)  1.54 us
  transfers between devices with their start and end apart: 1, of which 1 were waited for; matrix products, arithmetic and copies ran while one was open for 0% of the time, Pallas kernels for 6%

profile of v10, /device:TPU:1, one launch (start us, length us, event | category | flops | bytes accessed | tf_op | source)
XLA Modules:
  0.0 50.2 jit_solution(8946207130393061269)
XLA Ops:
  0.0 1.7 %shard_map.65 = bf16[256,128]{1,0:T(8,128)(2,1)} custom-call(s32[8,128]{1,0:T(8,128)} %bitcast.11, s32[8,128]{1,0:T(8,128)} %bitcast.13, bf16[16,320]{1,0:T(8,128)(2,1)} %queries_hbm.3, bf16[16,160]{1,0:T(8,128)(2,1)} %fresh_hbm.3), custom_call_target="tpu_custom_call" | custom-call | tf_op jit(solution)/shard_map/pallas_call | solution.py:338
  1.7 16.4 %all-to-all-start = ((bf16[64,4,128]{2,1,0:T(4,128)(2,1)}), bf16[64,4,128]{2,1,0:T(4,128)(2,1)S(1)}, u32[]{:S(2)}, u32[]{:S(2)}) async-start(bf16[64,4,128]{2,1,0:T(4,128)(2,1)} %bitcast.3), calls=%async_computation | async-start | bytes 131072 | tf_op jit(solution)/shard_map/all_to_all | solution.py:325
  18.1 2.9 %shard_map.64 = (bf16[160,6400]{1,0:T(8,128)(2,1)S(1)}, bf16[256,2560]{1,0:T(8,128)(2,1)S(1)}, f32[40,128]{1,0:T(8,128)S(1)}, bf16[256,128]{1,0:T(8,128)(2,1)S(1...) custom-call(s32[8,128]{1,0:T(8,128)} %bitcast.12, s32[8,128]{1,0:T(8,128)} %bitcast.14, ...), custom_call_target="tpu_custom_call" | custom-call | tf_op jit(solution)/shard_map/pallas_call | solution.py:338
  21.0 1.5 %all-to-all-done = bf16[64,4,128]{2,1,0:T(4,128)(2,1)S(1)} async-done(((bf16[64,4,128]{2,1,0:T(4,128)(2,1)}), bf16[64,4,128]{2,1,0:T(4,128)(2,1)S(1)}, u32[]{:S(2)}, u32[]{:S(2)}) %all-to-all-start) | async-done | bytes 65568 | tf_op jit(solution)/shard_map/all_to_all | solution.py:325
  22.5 2.1 %shard_map.66 = bf16[8,40,128]{2,1,0:T(8,128)(2,1)S(1)} custom-call(bf16[256,128]{1,0:T(8,128)(2,1)S(1)} %bitcast.7, bf16[32,256]{1,0:T(8,128)(2,1)S(1)} %get-tuple-element.14.chosen_t_ref, f32[40,128]{1,0:T(8,128)S(1)} %get-tuple-element.15.home_ref, bf16[160,6400]{1,0:T(8,128)(2,1)S(1)} %get-tuple-element.16.near_ref, ...), custom_call_target="tpu_custom_call" | custom-call | tf_op jit(solution)/shard_map/pallas_call | solution.py:338
  24.7 10.6 %all_to_all.15.shares_ref = bf16[8,40,128]{2,1,0:T(8,128)(2,1)S(1)} all-to-all(bf16[8,40,128]{2,1,0:T(8,128)(2,1)S(1)} %shard_map.66), channel_id=1, replica_groups={{5,1,2,0,3,7,4,6},{13,9,10,8,11,15,12,14},{21,17,18,16,19,23,20,22},{29..., dimensions={0} | all-to-all | bytes 163840 | tf_op jit(solution)/shard_map/all_to_all | solution.py:325
  35.3 0.1 shard_map.67
  35.5 13.9 %all_to_all.16 = bf16[64,4,128]{2,1,0:T(4,128)(2,1)S(1)} all-to-all(bf16[64,4,128]{2,1,0:T(4,128)(2,1)S(1)} %bitcast.9), channel_id=1, replica_groups={{424,128,136,176,184,144,152,160,168,64,72,112,120,80,88,96,104,192,200..., dimensions={0} | all-to-all | bytes 131072 | tf_op jit(solution)/shard_map/all_to_all | solution.py:325
  49.4 0.8 %shard_map.68 = bf16[16,320]{1,0:T(8,128)(2,1)} custom-call(bf16[32,256]{1,0:T(8,128)(2,1)S(1)} %get-tuple-element.13.placed_t_ref, f32[40,128]{1,0:T(8,128)S(1)} %get-tuple-element.19.home_ref, bf16[256,128]{1,0:T(8,128)(2,1)S(1)} %bitcast.8), custom_call_target="tpu_custom_call" | custom-call | tf_op jit(solution)/shard_map/pallas_call | solution.py:338
Async XLA Ops:
  1.7 20.8 %all-to-all-start = ((bf16[64,4,128]{2,1,0:T(4,128)(2,1)}), bf16[64,4,128]{2,1,0:T(4,128)(2,1)S(1)}, u32[]{:S(2)}, u32[]{:S(2)}) async-start(bf16[64,4,128]{2,1,0:T(4,128)(2,1)} %bitcast.3), calls=%async_computation | async-start | bytes 131072 | tf_op jit(solution)/shard_map/all_to_all | solution.py:325

commit v11 on v9

--- a/solution.py
+++ b/solution.py
@@ -101,8 +101,8 @@
 
 
 def send_kernel(
-    tokens, offsets_hbm, lengths_hbm, queries_hbm, fresh_hbm, out_ref,
-    offsets_ref, lengths_ref, queries_ref, fresh_ref, sems,
+    tokens, offsets_hbm, lengths_hbm, queries_hbm, fresh_hbm, out_hbm,
+    offsets_ref, lengths_ref, queries_ref, fresh_ref, out_ref, sems, out_sems,
 ):
     sources = (offsets_hbm, lengths_hbm, queries_hbm, fresh_hbm)
     for copy in fetch(sources, (offsets_ref, lengths_ref, queries_ref, fresh_ref), sems):
@@ -127,7 +127,15 @@
     fresh = fresh_ref[...].astype(F32)
     stack = pack(queries[8:], fresh[8:], starts, lengths)
     stack = jnp.concatenate([stack, jnp.zeros((96, LANES), F32)], axis=0)
-    out_ref[...] = dot(placed, stack.astype(BF)).astype(BF)
+    stack = stack.astype(BF)
+    copies = []
+    for i in range(2):
+        part = pl.ds(i * rows // 2, rows // 2)
+        out_ref[part] = dot(placed[i * rows // 2 : (i + 1) * rows // 2], stack).astype(BF)
+        copies.append(pltpu.make_async_copy(out_ref.at[part], out_hbm.at[part], out_sems.at[i]))
+        copies[i].start()
+    for copy in copies:
+        copy.wait()
 
 
 def weigh(queries, keys, values, inside, own, own_value):
@@ -359,12 +367,14 @@
     scratch = lambda x: pltpu.VMEM(x.shape, x.dtype)
     semaphores = pltpu.SemaphoreType.DMA
     inputs = (offsets, lengths, queries, fresh_kv)
-    (message,) = call(
+    (message,) = pl.pallas_call(
         functools.partial(send_kernel, tokens),
-        [slots],
-        far_args=inputs,
-        scratch=[*map(scratch, inputs), semaphores((4,))],
-    )
+        out_shape=[slots],
+        in_specs=[ANYWHERE] * 4,
+        out_specs=[pl.BlockSpec(memory_space=pltpu.HBM)],
+        scratch_shapes=[*map(scratch, inputs), scratch(slots), semaphores((4,)), semaphores((2,))],
+        compiler_params=pltpu.CompilerParams(vmem_limit_bytes=16 << 20),
+    )(*(in_hbm(a) for a in inputs))
     got = exchange(message.reshape(devices, 4, LANES), "req", req_group)
     near_blocks = (tokens - LMAX) // LANES + 1
     upper = out_weight.shape[0] * 4 // 5

time: 50.4 us -> 50.5 us (level)
    pallas_call x0 -> x1, Pallas kernels: none -> 1.72 us  [shards(): pl.pallas_call(functools.partial(send_kernel, tokens), out_shape=[slots],...]
    pallas_call x5 -> x4, Pallas kernels: 7.71 us -> 6 us  [call(): pl.pallas_call(kernel, out_shape=outs, in_specs=[NEAR] * len(args) + [ANY...]
where the time goes in v11:
time: 50.5 us; the launch traced here: 50.1 us
  blocking collectives  24.5 us (49%)
  starting transfers between devices  16.4 us (32%)
  Pallas kernels  7.73 us (15%)
  waiting for transfers between devices  1.54 us (3%)
    all_to_all x2, blocking collectives, exchange(): return lax.all_to_all(x, axis, 0, 0, axis_index_groups=[group], tiled=True)  24.5 us
    all_to_all x1, starting transfers between devices, exchange(): return lax.all_to_all(x, axis, 0, 0, axis_index_groups=[group], tiled=True)  16.4 us
    pallas_call x4, Pallas kernels, call(): pl.pallas_call(kernel, out_shape=outs, in_specs=[NEAR] * len(args) + [ANY...  6 us
    pallas_call x1, Pallas kernels, shards(): pl.pallas_call(functools.partial(send_kernel, tokens), out_shape=[slots],...  1.72 us
    all_to_all x1, waiting for transfers between devices, exchange(): return lax.all_to_all(x, axis, 0, 0, axis_index_groups=[group], tiled=True)  1.54 us
  transfers between devices with their start and end apart: 1, of which 1 were waited for; matrix products, arithmetic and copies ran while one was open for 0% of the time, Pallas kernels for 6%

profile of v11, /device:TPU:1, one launch (start us, length us, event | category | flops | bytes accessed | tf_op | source)
XLA Modules:
  0.0 50.1 jit_solution(18121206162454775862)
XLA Ops:
  0.0 1.7 %shard_map.65 = bf16[256,128]{1,0:T(8,128)(2,1)} custom-call(s32[8,128]{1,0:T(8,128)} %bitcast.11, s32[8,128]{1,0:T(8,128)} %bitcast.13, bf16[16,320]{1,0:T(8,128)(2,1)} %queries_hbm.3, bf16[16,160]{1,0:T(8,128)(2,1)} %fresh_hbm.3), custom_call_target="tpu_custom_call" | custom-call | tf_op jit(solution)/shard_map/pallas_call | solution.py:370
  1.7 16.4 %all-to-all-start = ((bf16[64,4,128]{2,1,0:T(4,128)(2,1)}), bf16[64,4,128]{2,1,0:T(4,128)(2,1)S(1)}, u32[]{:S(2)}, u32[]{:S(2)}) async-start(bf16[64,4,128]{2,1,0:T(4,128)(2,1)} %bitcast.3), calls=%async_computation | async-start | bytes 131072 | tf_op jit(solution)/shard_map/all_to_all | solution.py:333
  18.1 2.9 %shard_map.64 = (bf16[160,6400]{1,0:T(8,128)(2,1)S(1)}, bf16[256,2560]{1,0:T(8,128)(2,1)S(1)}, f32[40,128]{1,0:T(8,128)S(1)}, bf16[256,128]{1,0:T(8,128)(2,1)S(1...) custom-call(s32[8,128]{1,0:T(8,128)} %bitcast.12, s32[8,128]{1,0:T(8,128)} %bitcast.14, ...), custom_call_target="tpu_custom_call" | custom-call | tf_op jit(solution)/shard_map/pallas_call | solution.py:346
  21.0 1.5 %all-to-all-done = bf16[64,4,128]{2,1,0:T(4,128)(2,1)S(1)} async-done(((bf16[64,4,128]{2,1,0:T(4,128)(2,1)}), bf16[64,4,128]{2,1,0:T(4,128)(2,1)S(1)}, u32[]{:S(2)}, u32[]{:S(2)}) %all-to-all-start) | async-done | bytes 65568 | tf_op jit(solution)/shard_map/all_to_all | solution.py:333
  22.5 2.1 %shard_map.66 = bf16[8,40,128]{2,1,0:T(8,128)(2,1)S(1)} custom-call(bf16[256,128]{1,0:T(8,128)(2,1)S(1)} %bitcast.7, bf16[32,256]{1,0:T(8,128)(2,1)S(1)} %get-tuple-element.14.chosen_t_ref, f32[40,128]{1,0:T(8,128)S(1)} %get-tuple-element.15.home_ref, bf16[160,6400]{1,0:T(8,128)(2,1)S(1)} %get-tuple-element.16.near_ref, ...), custom_call_target="tpu_custom_call" | custom-call | tf_op jit(solution)/shard_map/pallas_call | solution.py:346
  24.7 10.7 %all_to_all.15.shares_ref = bf16[8,40,128]{2,1,0:T(8,128)(2,1)S(1)} all-to-all(bf16[8,40,128]{2,1,0:T(8,128)(2,1)S(1)} %shard_map.66), channel_id=1, replica_groups={{4,5,6,7,0,1,2,3},{12,13,14,15,8,9,10,11},{20,21,22,23,16,17,18,19},{28..., dimensions={0} | all-to-all | bytes 163840 | tf_op jit(solution)/shard_map/all_to_all | solution.py:333
  35.4 0.1 shard_map.67
  35.5 13.8 %all_to_all.16 = bf16[64,4,128]{2,1,0:T(4,128)(2,1)S(1)} all-to-all(bf16[64,4,128]{2,1,0:T(4,128)(2,1)S(1)} %bitcast.9), channel_id=1, replica_groups={{424,128,136,176,184,144,152,160,168,64,72,112,120,80,88,96,104,192,200..., dimensions={0} | all-to-all | bytes 131072 | tf_op jit(solution)/shard_map/all_to_all | solution.py:333
  49.3 0.8 %shard_map.68 = bf16[16,320]{1,0:T(8,128)(2,1)} custom-call(bf16[32,256]{1,0:T(8,128)(2,1)S(1)} %get-tuple-element.13.placed_t_ref, f32[40,128]{1,0:T(8,128)S(1)} %get-tuple-element.19.home_ref, bf16[256,128]{1,0:T(8,128)(2,1)S(1)} %bitcast.8), custom_call_target="tpu_custom_call" | custom-call | tf_op jit(solution)/shard_map/pallas_call | solution.py:346
Async XLA Ops:
  1.7 20.8 %all-to-all-start = ((bf16[64,4,128]{2,1,0:T(4,128)(2,1)}), bf16[64,4,128]{2,1,0:T(4,128)(2,1)S(1)}, u32[]{:S(2)}, u32[]{:S(2)}) async-start(bf16[64,4,128]{2,1,0:T(4,128)(2,1)} %bitcast.3), calls=%async_computation | async-start | bytes 131072 | tf_op jit(solution)/shard_map/all_to_all | solution.py:333

commit v12 on v11

--- a/solution.py
+++ b/solution.py
@@ -15,7 +15,7 @@
 LANES = 128
 HALF = 8
 FIRST_Z, FIRST_X, FIRST_CORE = 6, 2, 1
-TP_FIRST = 4
+TP_FIRST = 5
 BF = jnp.bfloat16
 F32 = jnp.float32
 I32 = jnp.int32

time: 50.5 us -> 50.4 us (level)
  no operation moved by 1% of the time
where the time goes in v12:
time: 50.4 us; the launch traced here: 50.1 us
  blocking collectives  24.4 us (48%)
  starting transfers between devices  16.4 us (33%)
  Pallas kernels  7.73 us (15%)
  waiting for transfers between devices  1.54 us (3%)
    all_to_all x2, blocking collectives, exchange(): return lax.all_to_all(x, axis, 0, 0, axis_index_groups=[group], tiled=True)  24.4 us
    all_to_all x1, starting transfers between devices, exchange(): return lax.all_to_all(x, axis, 0, 0, axis_index_groups=[group], tiled=True)  16.4 us
    pallas_call x4, Pallas kernels, call(): pl.pallas_call(kernel, out_shape=outs, in_specs=[NEAR] * len(args) + [ANY...  6 us
    pallas_call x1, Pallas kernels, shards(): pl.pallas_call(functools.partial(send_kernel, tokens), out_shape=[slots],...  1.72 us
    all_to_all x1, waiting for transfers between devices, exchange(): return lax.all_to_all(x, axis, 0, 0, axis_index_groups=[group], tiled=True)  1.54 us
  transfers between devices with their start and end apart: 1, of which 1 were waited for; matrix products, arithmetic and copies ran while one was open for 0% of the time, Pallas kernels for 6%

profile of v12, /device:TPU:1, one launch (start us, length us, event | category | flops | bytes accessed | tf_op | source)
XLA Modules:
  0.0 50.1 jit_solution(15940417523727054642)
XLA Ops:
  0.0 1.7 %shard_map.65 = bf16[256,128]{1,0:T(8,128)(2,1)} custom-call(s32[8,128]{1,0:T(8,128)} %bitcast.11, s32[8,128]{1,0:T(8,128)} %bitcast.13, bf16[16,320]{1,0:T(8,128)(2,1)} %queries_hbm.3, bf16[16,160]{1,0:T(8,128)(2,1)} %fresh_hbm.3), custom_call_target="tpu_custom_call" | custom-call | tf_op jit(solution)/shard_map/pallas_call | solution.py:370
  1.7 16.4 %all-to-all-start = ((bf16[64,4,128]{2,1,0:T(4,128)(2,1)}), bf16[64,4,128]{2,1,0:T(4,128)(2,1)S(1)}, u32[]{:S(2)}, u32[]{:S(2)}) async-start(bf16[64,4,128]{2,1,0:T(4,128)(2,1)} %bitcast.3), calls=%async_computation | async-start | bytes 131072 | tf_op jit(solution)/shard_map/all_to_all | solution.py:333
  18.1 2.9 %shard_map.64 = (bf16[160,6400]{1,0:T(8,128)(2,1)S(1)}, bf16[256,2560]{1,0:T(8,128)(2,1)S(1)}, f32[40,128]{1,0:T(8,128)S(1)}, bf16[256,128]{1,0:T(8,128)(2,1)S(1...) custom-call(s32[8,128]{1,0:T(8,128)} %bitcast.12, s32[8,128]{1,0:T(8,128)} %bitcast.14, ...), custom_call_target="tpu_custom_call" | custom-call | tf_op jit(solution)/shard_map/pallas_call | solution.py:346
  21.0 1.5 %all-to-all-done = bf16[64,4,128]{2,1,0:T(4,128)(2,1)S(1)} async-done(((bf16[64,4,128]{2,1,0:T(4,128)(2,1)}), bf16[64,4,128]{2,1,0:T(4,128)(2,1)S(1)}, u32[]{:S(2)}, u32[]{:S(2)}) %all-to-all-start) | async-done | bytes 65568 | tf_op jit(solution)/shard_map/all_to_all | solution.py:333
  22.5 2.1 %shard_map.66 = bf16[8,40,128]{2,1,0:T(8,128)(2,1)S(1)} custom-call(bf16[256,128]{1,0:T(8,128)(2,1)S(1)} %bitcast.7, bf16[32,256]{1,0:T(8,128)(2,1)S(1)} %get-tuple-element.14.chosen_t_ref, f32[40,128]{1,0:T(8,128)S(1)} %get-tuple-element.15.home_ref, bf16[160,6400]{1,0:T(8,128)(2,1)S(1)} %get-tuple-element.16.near_ref, ...), custom_call_target="tpu_custom_call" | custom-call | tf_op jit(solution)/shard_map/pallas_call | solution.py:346
  24.7 10.7 %all_to_all.15.shares_ref = bf16[8,40,128]{2,1,0:T(8,128)(2,1)S(1)} all-to-all(bf16[8,40,128]{2,1,0:T(8,128)(2,1)S(1)} %shard_map.66), channel_id=1, replica_groups={{5,6,7,0,1,2,3,4},{13,14,15,8,9,10,11,12},{21,22,23,16,17,18,19,20},{29..., dimensions={0} | all-to-all | bytes 163840 | tf_op jit(solution)/shard_map/all_to_all | solution.py:333
  35.5 0.1 shard_map.67
  35.6 13.7 %all_to_all.16 = bf16[64,4,128]{2,1,0:T(4,128)(2,1)S(1)} all-to-all(bf16[64,4,128]{2,1,0:T(4,128)(2,1)S(1)} %bitcast.9), channel_id=1, replica_groups={{424,128,136,176,184,144,152,160,168,64,72,112,120,80,88,96,104,192,200..., dimensions={0} | all-to-all | bytes 131072 | tf_op jit(solution)/shard_map/all_to_all | solution.py:333
  49.3 0.8 %shard_map.68 = bf16[16,320]{1,0:T(8,128)(2,1)} custom-call(bf16[32,256]{1,0:T(8,128)(2,1)S(1)} %get-tuple-element.13.placed_t_ref, f32[40,128]{1,0:T(8,128)S(1)} %get-tuple-element.19.home_ref, bf16[256,128]{1,0:T(8,128)(2,1)S(1)} %bitcast.8), custom_call_target="tpu_custom_call" | custom-call | tf_op jit(solution)/shard_map/pallas_call | solution.py:346
Async XLA Ops:
  1.7 20.8 %all-to-all-start = ((bf16[64,4,128]{2,1,0:T(4,128)(2,1)}), bf16[64,4,128]{2,1,0:T(4,128)(2,1)S(1)}, u32[]{:S(2)}, u32[]{:S(2)}) async-start(bf16[64,4,128]{2,1,0:T(4,128)(2,1)} %bitcast.3), calls=%async_computation | async-start | bytes 131072 | tf_op jit(solution)/shard_map/all_to_all | solution.py:333
